TPU v7x, 512 devices: a whole 4x4x16 slice. The times are simulated.
512 devices in a mesh: replica: 32 (over z, core), tensor: 16 (over x, y).
Axes of the slice: x: 4, y: 4, z: 16, core: 2. Of those that a mesh axis runs over, the one named last changes fastest.
Arguments:
- x_input: bfloat16 [8192, 4096], P('replica', 'tensor'), may hold values from -6 to 6
- z_input: bfloat16 [8192, 4096], P('replica', 'tensor'), may hold values from -6 to 6
- bc_input: bfloat16 [8192, 1024], P('replica'), may hold values from -6 to 6
- dt_raw: float32 [8192, 128], P('replica', 'tensor'), may hold values from -6 to 6
- dt_bias: float32 [128], P('tensor'), may hold values from -3 to -1
- decay_rates: float32 [128], P('tensor'), may hold values from 0.005 to 0.5
- skip_gain: float32 [128], P('tensor'), may hold values from 0.5 to 1.5
- conv_x: float32 [4, 4096], P(None, 'tensor'), may hold values from -3 to 3
- conv_bc: float32 [4, 1024], replicated, may hold values from -3 to 3
- norm_gain: float32 [4096], P('tensor'), may hold values from 0.5 to 1.5
- out_weight: bfloat16 [4096, 4096], P('tensor'), may hold values from -0.09375 to 0.09375
- cached_states: float32 [64, 128, 32, 128], P('replica', 'tensor'), may hold values from -4 to 4
- cached_tail_x: float32 [64, 3, 4096], P('replica', None, 'tensor'), may hold values from -6 to 6
- cached_tail_bc: float32 [64, 3, 1024], P('replica'), may hold values from -6 to 6
- prefix_block: int32 [64], replicated, may hold values from 0 to 63, as said below
- lengths: int32 [64], P('replica'), may hold values from 128 to 128, as said below
Outputs:
- mixed: bfloat16 [8192, 4096], P(('replica', 'tensor'))
- final_states: float32 [64, 128, 32, 128], P('replica', 'tensor')
Inputs may be any that keep to these rules, and one draw needn't show every extreme that they name: A permutation: request q (on replica q // 2) starts from cached block prefix_block[q], which replica prefix_block[q] // 2 holds; every cached block feeds exactly one request. `lengths`: every request's suffix fills all 128 of its slots, so every entry is 128.
All inputs are finite; a program needn't handle non-finite values.
Results may differ from a plain program's by a relative error of at most 0.015.
Values may be sent and summed in bfloat16 or wider, within the bound.
A program may use at most 64 MiB of HBM per device.

v0:
```python
import jax
import jax.numpy as jnp
from jax import lax
from jax.sharding import PartitionSpec as P

HEADS = 128
HEAD_DIM = 32
STATE = 128
GROUPS = 4


highest = lax.Precision.HIGHEST
epsilon = 1e-05


def causal_conv(tail_rows, sequence, kernel):
    joined = jnp.concatenate([tail_rows, sequence], axis=0)
    length = sequence.shape[0]
    total = joined[0:length] * kernel[0][None, :]
    for offset in range(1, kernel.shape[0]):
        total = total + joined[offset : offset + length] * kernel[offset][None, :]
    return jax.nn.silu(total)


def span_scan(inputs, b_heads, c_heads, step_sizes, decay_rates, skip_gain, carry_state):
    logdec = -step_sizes * decay_rates[None, :]
    cumulative = jnp.cumsum(logdec, axis=0)
    count_rows = inputs.shape[0]
    causal = jnp.arange(count_rows)[:, None] >= jnp.arange(count_rows)[None, :]
    cum_heads = jnp.transpose(cumulative)
    differ = cum_heads[:, :, None] - cum_heads[:, None, :]
    decays = jnp.where(causal[None, :, :], jnp.exp(jnp.minimum(differ, 0.0)), 0.0)
    scores = jnp.einsum("ihn,jhn->hij", c_heads, b_heads, precision=highest)
    weights = scores * decays * jnp.transpose(step_sizes)[:, None, :]
    inside = jnp.einsum("hij,jhp->ihp", weights, inputs, precision=highest)
    carried = jnp.exp(cumulative)[:, :, None] * jnp.einsum(
        "ihn,hpn->ihp", c_heads, carry_state, precision=highest
    )
    output = inside + carried + skip_gain[None, :, None] * inputs
    ending = cumulative[-1]
    weigh_in = jnp.exp(ending[None, :] - cumulative) * step_sizes
    new_state = jnp.exp(ending)[:, None, None] * carry_state + jnp.einsum(
        "jh,jhp,jhn->hpn", weigh_in, inputs, b_heads, precision=highest
    )
    return (output, new_state)


def local(
    x_input,
    z_input,
    bc_input,
    dt_raw,
    dt_bias,
    decay_rates,
    skip_gain,
    conv_x,
    conv_bc,
    norm_gain,
    out_weight,
    cached_states,
    cached_tail_x,
    cached_tail_bc,
    prefix_block,
    lengths,
):
    requests = lengths.shape[0]
    local_heads = dt_raw.shape[1]
    tokens_dev = x_input.shape[0]
    slot_len = tokens_dev // requests
    wanted = lax.dynamic_slice_in_dim(prefix_block, lax.axis_index("replica") * requests, requests)
    empty_carry = (
        jnp.zeros_like(cached_states),
        jnp.zeros_like(cached_tail_x),
        jnp.zeros_like(cached_tail_bc),
    )
    pick_pieces = (
        lax.all_gather(cached_states.astype(jnp.bfloat16), "replica", axis=0, tiled=True).astype(
            jnp.float32
        ),
        lax.all_gather(cached_tail_x.astype(jnp.bfloat16), "replica", axis=0, tiled=True).astype(
            jnp.float32
        ),
        lax.all_gather(cached_tail_bc.astype(jnp.bfloat16), "replica", axis=0, tiled=True).astype(
            jnp.float32
        ),
    )
    count_blocks = pick_pieces[0].shape[0]
    inside = (wanted >= 0) & (wanted < count_blocks)
    position = jnp.clip(wanted, 0, count_blocks - 1)
    chosen = []
    for current, piece in zip(empty_carry, pick_pieces):
        taken_rows = jnp.take(piece, position, axis=0)
        in_mask = inside.reshape((requests,) + (1,) * (current.ndim - 1))
        chosen.append(jnp.where(in_mask, taken_rows, current))
    start_states, start_tail_x, start_tail_bc = tuple(chosen)
    head_ids = lax.axis_index("tensor") * local_heads + jnp.arange(local_heads)
    member = ((head_ids // (HEADS // GROUPS))[:, None] == jnp.arange(GROUPS)[None, :]).astype(
        jnp.float32
    )
    live = jnp.arange(slot_len)[None, :] < lengths[:, None]
    outputs = []
    finals = []
    for request in range(requests):
        row_lo = request * slot_len
        row_hi = row_lo + slot_len
        inputs = causal_conv(
            start_tail_x[request], x_input[row_lo:row_hi].astype(jnp.float32), conv_x
        ).reshape(slot_len, local_heads, HEAD_DIM)
        bc_conv = causal_conv(
            start_tail_bc[request], bc_input[row_lo:row_hi].astype(jnp.float32), conv_bc
        )
        b_groups = bc_conv[:, : GROUPS * STATE].reshape(slot_len, GROUPS, STATE)
        c_groups = bc_conv[:, GROUPS * STATE :].reshape(slot_len, GROUPS, STATE)
        b_heads = jnp.einsum("lgn,hg->lhn", b_groups, member, precision=highest)
        c_heads = jnp.einsum("lgn,hg->lhn", c_groups, member, precision=highest)
        step_sizes = jnp.where(
            live[request][:, None], jax.nn.softplus(dt_raw[row_lo:row_hi] + dt_bias[None, :]), 0.0
        )
        carry_state = start_states[request]
        output, carry_state = span_scan(
            inputs, b_heads, c_heads, step_sizes, decay_rates, skip_gain, carry_state
        )
        outputs.append(output.reshape(slot_len, -1))
        finals.append(carry_state)
    outputs = jnp.concatenate(outputs, axis=0)
    final_states = jnp.stack(finals, axis=0)
    gate_vals = outputs * jax.nn.silu(z_input.astype(jnp.float32))
    by_head = gate_vals.reshape(tokens_dev, local_heads, HEAD_DIM)
    head_squares = jnp.sum(by_head * by_head, axis=2)
    partial_sq = jnp.dot(head_squares, member, precision=highest)
    totals = lax.psum(partial_sq, "tensor")
    mean_sq = jnp.dot(totals, jnp.transpose(member), precision=highest) / (
        HEADS * HEAD_DIM // GROUPS
    )
    normed = (by_head * lax.rsqrt(mean_sq + epsilon)[:, :, None]).reshape(
        tokens_dev, -1
    ) * norm_gain[None, :]
    gated = jnp.where(live.reshape(tokens_dev, 1), normed, 0.0).astype(jnp.bfloat16)
    mixed = lax.psum_scatter(
        jnp.dot(gated, out_weight, preferred_element_type=jnp.float32).astype(jnp.bfloat16),
        "tensor",
        scatter_dimension=0,
        tiled=True,
    )
    return (mixed, final_states)


def solution(mesh):
    placed = (
        P("replica", "tensor"),
        P("replica", "tensor"),
        P("replica", None),
        P("replica", "tensor"),
        P("tensor"),
        P("tensor"),
        P("tensor"),
        P(None, "tensor"),
        P(),
        P("tensor"),
        P("tensor", None),
        P("replica", "tensor", None, None),
        P("replica", None, "tensor"),
        P("replica", None, None),
        P(),
        P("replica"),
    )
    return jax.shard_map(
        local,
        mesh=mesh,
        in_specs=placed,
        out_specs=(P(("replica", "tensor"), None), P("replica", "tensor", None, None)),
        check_vma=False,
    )
```

profile of v0, /device:TPU:1, one launch (start us, length us, event | category | flops | bytes accessed | tf_op | source)
XLA Modules:
  0.0 260.8 jit_solution(10844467314238256731)
XLA Ops:
  7.2 1.8 convert_element_type.46
  9.1 1.3 fusion.71
  10.4 0.8 negate_multiply_fusion.1
  11.5 0.7 copy.104
  12.2 0.6 exp.69
  13.1 0.7 copy.106
  13.8 0.6 exp.74
  14.4 0.7 convert_element_type.43
  15.1 39.2 %all_gather.10 = bf16[64,3,1024]{2,1,0:T(4,128)(2,1)S(1)} all-gather(bf16[2,3,1024]{2,1,0:T(4,128)(2,1)S(1)} %copy.87), channel_id=1, replica_groups=mesh['replica'=32,'tensor'=16] {'replica'}, dimensions={0}, use_global_device_ids=true | all-gather | bytes 405504 | tf_op jit(solution)/shard_map/all_gather | solution.py:83
  55.3 1.2 slice_convert_fusion.1
  56.5 0.6 divide_multiply_fusion.1
  57.1 0.8 fusion.79
  57.9 1.0 reshape.120
  59.0 27.5 %all_gather.9 = bf16[64,3,256]{2,1,0:T(4,128)(2,1)S(1)} all-gather(bf16[2,3,256]{2,1,0:T(4,128)(2,1)S(1)} %copy.85), channel_id=1, replica_groups=mesh['replica'=32,'tensor'=16] {'replica'}, dimensions={0}, use_global_device_ids=true | all-gather | bytes 101376 | tf_op jit(solution)/shard_map/all_gather | solution.py:80
  86.5 0.7 convert_element_type.41
  87.2 1.6 gather_fusion
  89.0 0.9 slice_convert_fusion.3
  89.9 0.9 divide_multiply_fusion.3
  90.7 1.0 copy.86
  91.7 0.8 reshape.124
  92.5 1.0 copy.95
  93.5 0.8 reshape.119
  94.4 1.5 copy.93
  95.9 0.8 reshape.123
  96.7 1.5 copy.101
  98.3 1.7 copy.103
  100.0 1.4 exponential_multiply_fusion.1
  101.9 1.4 convolution_bitcast_fusion.3
  103.3 1.3 fusion.1
  104.6 1.6 convolution_bitcast_fusion.7
  106.2 1.4 convolution_bitcast_fusion
  108.0 1.3 fusion
  109.3 1.6 convolution_bitcast_fusion.5
  110.9 6.6 %convert_element_type.47 = f32[64,8,32,128]{3,2,1,0:T(8,128)} convert(bf16[64,8,32,128]{3,2,1,0:T(8,128)(2,1)} %all-gather.2.cloned.1.call-done) | non-fusion elementwise | flops 2097152 | bytes 12582912 | tf_op jit(solution)/shard_map/convert_element_type | solution.py:77
  117.6 4.8 %gather_fusion.2 = f32[2,8,32,128]{3,2,1,0:T(8,128)} fusion(f32[64,8,32,128]{3,2,1,0:T(8,128)} %convert_element_type.47, s32[1024]{0:T(1024)} %copy-done.18), kind=kCustom, calls=%fused_computation.2 | custom fusion | bytes 524296 | tf_op jit(solution)/shard_map/jit(_take)/gather | solution.py:92
  122.3 1.1 select_select_fusion
  123.4 2.1 fusion.9
  125.5 2.1 fusion.6
  127.6 0.8 bitcast_reduce_fusion
  128.5 34.0 %psum.7 = f32[256,4]{0,1:T(4,128)} all-reduce(f32[256,4]{0,1:T(4,128)S(1)} %fusion.65), channel_id=1, replica_groups=mesh['replica'=32,'tensor'=16] {'tensor'}, use_global_device_ids=true, to_apply=%region_3.4 | all-reduce | flops 1024 | bytes 8192 | tf_op jit(solution)/shard_map/psum | solution.py:131
  162.5 0.9 fusion.11
  163.4 1.1 fusion.42
  164.5 2.1 convolution_convert_fusion
  166.6 0.7 fusion.69
  167.3 0.7 fusion.70
  168.0 1.5 fusion.3
  170.1 0.7 pad_maximum_fusion.2
  170.8 83.2 %reduce-scatter.2.cloned.1.call-done = bf16[16,4096]{1,0:T(8,128)(2,1)} async-done(((bf16[256,4096]{1,0:T(8,128)(2,1)}), bf16[16,4096]{1,0:T(8,128)(2,1)}) %reduce-scatter.2.cloned.1.call-update) | async-done | bytes 131088 | tf_op jit(solution)/shard_map/reduce_scatter | solution.py:139
  (80 shorter events, 3.5 us)
Async XLA Ops:
  7.2 157.3 %copy-start = (bf16[256,4096]{1,0:T(8,128)(2,1)S(1)}, bf16[256,4096]{1,0:T(8,128)(2,1)}, u32[]{:S(2)}) copy-start(bf16[256,4096]{1,0:T(8,128)(2,1)} %param.26) | copy-start | bytes 6291460
  7.2 47.3 %copy-start.23 = (s32[64]{0:T(128)S(1)}, s32[64]{0:T(128)}, u32[]{:S(2)}) copy-start(s32[64]{0:T(128)} %param.30) | copy-start | bytes 772
  7.2 48.0 %copy-start.12 = (f32[4,1024]{1,0:T(4,128)S(1)}, f32[4,1024]{1,0:T(4,128)}, u32[]{:S(2)}) copy-start(f32[4,1024]{1,0:T(4,128)} %param.24) | copy-start | bytes 49156
  7.2 103.7 %all-gather.2.cloned.1.call-start = ((), (), s32[]{:S(2)}) async-start(), calls=%async_computation.1 | async-start | bytes 4325376 | tf_op jit(solution)/shard_map/all_gather | solution.py:77
  9.0 245.0 %reduce-scatter.2.cloned.1.call-start = ((), (), s32[]{:S(2)}) async-start(), calls=%async_computation.2 | async-start | bytes 2228224 | tf_op jit(solution)/shard_map/reduce_scatter | solution.py:139
  10.4 2.4 copy-start.20
  10.4 2.4 copy-start.21
  11.5 88.5 %copy-start.4 = (f32[128,8]{1,0:T(8,128)}, f32[128,8]{1,0:T(8,128)S(1)}, u32[]{:S(2)}) copy-start(f32[128,8]{1,0:T(8,128)S(1)} %reduce_window_sum.17) | copy-start | bytes 12292
  13.1 86.9 %copy-start.5 = (f32[128,8]{1,0:T(8,128)}, f32[128,8]{1,0:T(8,128)S(1)}, u32[]{:S(2)}) copy-start(f32[128,8]{1,0:T(8,128)S(1)} %reduce_window_sum.18) | copy-start | bytes 12292
  54.6 2.6 copy-start.16
  54.6 34.3 %copy-start.15 = (pred[2]{0:T(512)(128)(4,1)}, pred[2]{0:T(512)(128)(4,1)S(1)}, u32[]{:S(2)}) copy-start(pred[2]{0:T(512)(128)(4,1)S(1)} %get-tuple-element.4) | copy-start | bytes 10
  54.6 2.6 copy-start.18
  56.4 2.5 copy-start.19
  57.1 31.8 %copy-start.22 = (f32[4,256]{1,0:T(4,128)S(1)}, f32[4,256]{1,0:T(4,128)}, u32[]{:S(2)}) copy-start(f32[4,256]{1,0:T(4,128)} %param.23) | copy-start | bytes 12292
  57.1 31.7 %copy-start.17 = (pred[2]{0:T(512)(128)(4,1)S(1)}, pred[2]{0:T(512)(128)(4,1)}, u32[]{:S(2)}) copy-start(pred[2]{0:T(512)(128)(4,1)} %copy-done.16) | copy-start | bytes 10
  59.0 41.0 %copy-start.8 = (f32[256,8]{0,1:T(8,128)S(1)}, f32[256,8]{0,1:T(8,128)}, u32[]{:S(2)}) copy-start(f32[256,8]{0,1:T(8,128)} %param.19) | copy-start | bytes 24580
  91.7 12.8 %copy-start.3 = (f32[128,256]{0,1:T(8,128)}, f32[128,256]{0,1:T(8,128)S(1)}, u32[]{:S(2)}) copy-start(f32[128,256]{0,1:T(8,128)S(1)} %copy.86) | copy-start | bytes 393220
  99.9 7.6 %copy-start.13 = (s32[8]{0:T(128)}, s32[8]{0:T(128)S(1)}, u32[]{:S(2)}) copy-start(s32[8]{0:T(128)S(1)} %and_select_fusion) | copy-start | bytes 100
  101.9 5.7 %copy-start.6 = (f32[128,4,128]{2,1,0:T(4,128)S(1)}, f32[128,4,128]{2,1,0:T(4,128)}, u32[]{:S(2)}) copy-start(f32[128,4,128]{2,1,0:T(4,128)} %reshape.123) | copy-start | bytes 786436
  103.3 6.0 %copy-start.1 = (f32[128,8,128]{2,1,0:T(8,128)}, f32[128,8,128]{2,1,0:T(8,128)S(1)}, u32[]{:S(2)}) copy-start(f32[128,8,128]{2,1,0:T(8,128)S(1)} %convolution_bitcast_fusion.3) | copy-start | bytes 1572868
  108.0 1.3 copy-start.2
  110.9 12.5 %copy-start.10 = (f32[128,8]{0,1:T(8,128)S(1)}, f32[128,8]{0,1:T(8,128)}, u32[]{:S(2)}) copy-start(f32[128,8]{0,1:T(8,128)} %copy.93) | copy-start | bytes 12292
  117.5 8.0 %copy-start.11 = (f32[128,8]{0,1:T(8,128)S(1)}, f32[128,8]{0,1:T(8,128)}, u32[]{:S(2)}) copy-start(f32[128,8]{0,1:T(8,128)} %copy.101) | copy-start | bytes 12292
  117.6 10.8 %copy-start.14 = (s32[8]{0:T(128)S(1)}, s32[8]{0:T(128)}, u32[]{:S(2)}) copy-start(s32[8]{0:T(128)} %copy-done.13) | copy-start | bytes 100
  122.3 5.2 %copy-start.7 = (bf16[256,256]{0,1:T(8,128)(2,1)S(1)}, bf16[256,256]{0,1:T(8,128)(2,1)}, u32[]{:S(2)}) copy-start(bf16[256,256]{0,1:T(8,128)(2,1)} %copy.103) | copy-start | bytes 393220
  166.6 1.4 copy-start.9
Sparse Core Ops, SparseCore 0:
  10.1 79.6 all-gather.1
  166.7 87.2 reduce-scatter.1
where the time goes:
time: 262 us; the launch traced here: 261 us
  blocking collectives  101 us (39%)
  waiting for transfers between devices  83.2 us (32%)
  local copies, waits for them, and re-layouts  22.3 us (9%)
  other arithmetic  21.4 us (8%)
  matrix products  18.7 us (7%)
  between operations  14.5 us (6%)
    reduce_scatter x1, waiting for transfers between devices, local(): lax.psum_scatter(jnp.dot(gated, out_weight, preferred_element_type=jnp.fl...  83.2 us
    all_gather x1, blocking collectives, local(): lax.all_gather(cached_tail_bc.astype(jnp.bfloat16), 'replica', axis=0, ti...  39.2 us
    psum x1, blocking collectives, local(): totals = lax.psum(partial_sq, 'tensor')  34 us
    all_gather x1, blocking collectives, local(): lax.all_gather(cached_tail_x.astype(jnp.bfloat16), 'replica', axis=0, til...  27.5 us
    gather x3, local copies, waits for them, and re-layouts, local(): taken_rows = jnp.take(piece, position, axis=0)  6.99 us
    convert_element_type x1, other arithmetic, local(): lax.all_gather(cached_states.astype(jnp.bfloat16), 'replica', axis=0, til...  6.65 us
  transfers between devices with their start and end apart: 2, of which 1 were waited for; matrix products, arithmetic and copies ran while one was open for 15% of the time, Pallas kernels for 0%

commit v1 on v0

v1 whole, which is shorter than its diff:
```python
import functools

import jax
import jax.numpy as jnp
from jax import lax
from jax.experimental import pallas as pl
from jax.experimental.pallas import tpu as pltpu
from jax.sharding import PartitionSpec as P

MESH = pl.DeviceIdType.MESH
HIGHEST = lax.Precision.HIGHEST
F32 = jnp.float32
BF16 = jnp.bfloat16
HEAD_DIM = 32
STATE = 128
EPSILON = 1e-05
TAIL_ROWS = 12

NT_DIMS = (((1,), (1,)), ((), ()))
TN_DIMS = (((0,), (0,)), ((), ()))


def dot_nt(a, b, precision=None):
    return lax.dot_general(a, b, NT_DIMS, precision=precision, preferred_element_type=F32)


def dot_tn(a, b, precision=None):
    return lax.dot_general(a, b, TN_DIMS, precision=precision, preferred_element_type=F32)


def iota(shape, axis):
    return lax.broadcasted_iota(jnp.int32, shape, axis)


def silu(a):
    return a / (1.0 + jnp.exp(-a))


def layer_kernel(
    sizes,
    prefix_s,
    lengths_s,
    bias_s,
    rates_s,
    skip_s,
    x_h,
    z_h,
    bc_h,
    dt_h,
    convx_h,
    convbc_h,
    gain_h,
    weight_h,
    states_h,
    tailx_h,
    tailbc_h,
    mixed_o,
    final_o,
    x_v,
    z_v,
    bc_v,
    dt_v,
    convx_v,
    convbc_v,
    gain_v,
    st_v,
    tailx_v,
    tailbc_v,
    send1,
    recv1,
    send2,
    recv2,
    tsend1,
    trecv1,
    tsend2,
    trecv2,
    w_a,
    w_b,
    xraw,
    bcraw,
    gate,
    decay,
    expcum,
    weighin,
    ending,
    v_f,
    v_a,
    v_b,
    r_a,
    r_b,
    ss_send,
    ss_recv,
    o_a,
    o_b,
    ro_a,
    ro_b,
    load_sem,
    own_sem,
    s1_send,
    s1_recv,
    s2_send,
    s2_recv,
    t1_send,
    t1_recv,
    t2_send,
    t2_recv,
    w_send,
    w_recv,
    va_send,
    va_recv,
    vb_send,
    vb_recv,
    ss_ssem,
    ss_rsem,
    oa_send,
    oa_recv,
    ob_send,
    ob_recv,
):
    nr, nx, ny = sizes
    nz = nr // 2
    groups = nx
    tokens, width = x_v.shape
    heads = width // HEAD_DIM
    slot = tokens // 2
    rows_owner = tokens // (nx * ny)
    piece = width // nr
    tail_n = trecv2.shape[0]
    tail_p = TAIL_ROWS // tail_n
    quarter = w_a.shape[2]
    half_cols = 2 * quarter

    me_r = lax.axis_index("replica")
    me_t = lax.axis_index("tensor")
    zi, ci = me_r // 2, me_r % 2
    xi, yi = me_t // ny, me_t % ny

    def each_replica(fn):
        def step(m, carry):
            k = (m + 1) // 2
            dz = nz // 2 + k * (1 - 2 * (m % 2))
            zz = (zi + dz) % nz
            fn(zz * 2)
            fn(zz * 2 + 1)
            return carry

        lax.fori_loop(0, nz - 1, step, 0)
        fn(zi * 2 + 1 - ci)

    def y_peers():
        out = []
        for d in range(ny):
            for dc in range(2):
                if d or dc:
                    out.append(((yi + d) % ny, (ci + dc) % 2))
        return out

    def x_peers():
        out = []
        for d in range(nx):
            for dc in range(2):
                if d or dc:
                    out.append(((xi + d) % nx, (ci + dc) % 2))
        return out

    def tensor_of(xx, yy):
        return xx * ny + yy

    def remote(src, dst, ssem, rsem, rr, tt):
        return pltpu.make_async_remote_copy(
            src_ref=src,
            dst_ref=dst,
            send_sem=ssem,
            recv_sem=rsem,
            device_id=(rr, tt),
            device_id_type=MESH,
        )

    barrier = pltpu.get_barrier_semaphore()

    def greet(rr, tt):
        pl.semaphore_signal(barrier, inc=1, device_id=(rr, tt), device_id_type=MESH)

    each_replica(lambda rr: greet(rr, me_t))
    for d in range(1, ny):
        for cc in range(2):
            greet(zi * 2 + cc, tensor_of(xi, (yi + d) % ny))
    for d in range(1, nx):
        for cc in range(2):
            greet(zi * 2 + cc, tensor_of((xi + d) % nx, yi))
    expected = 2 * (nz - 1) + 1 + 2 * (ny - 1) + 2 * (nx - 1)

    b_lo = pl.multiple_of(xi * STATE, STATE)
    c_lo = pl.multiple_of((groups + xi) * STATE, STATE)
    cols_a = pl.ds(pl.multiple_of(ci * quarter, quarter), quarter)
    cols_b = pl.ds(pl.multiple_of(half_cols + ci * quarter, quarter), quarter)
    lane_b, lane_c = pl.ds(0, STATE), pl.ds(STATE, STATE)
    loads = []

    def load(src, dst):
        copy = pltpu.make_async_copy(src, dst, load_sem.at[len(loads)])
        copy.start()
        loads.append(copy)
        return copy

    load_states = load(states_h, st_v)
    load_tx = load(tailx_h, tailx_v)
    load_tb = load(tailbc_h.at[:, :, pl.ds(b_lo, STATE)], tailbc_v.at[:, :, lane_b])
    load_tc = load(tailbc_h.at[:, :, pl.ds(c_lo, STATE)], tailbc_v.at[:, :, lane_c])
    load_dt = load(dt_h, dt_v)
    load_x = load(x_h, x_v)
    load_b = load(bc_h.at[:, pl.ds(b_lo, STATE)], bc_v.at[:, lane_b])
    load_c = load(bc_h.at[:, pl.ds(c_lo, STATE)], bc_v.at[:, lane_c])
    load_cx = load(convx_h, convx_v)
    load_cb = load(convbc_h.at[:, pl.ds(b_lo, STATE)], convbc_v.at[:, lane_b])
    load_cc = load(convbc_h.at[:, pl.ds(c_lo, STATE)], convbc_v.at[:, lane_c])
    load_z = load(z_h, z_v)
    load_g = load(gain_h, gain_v)
    load_wa = load(weight_h.at[:, cols_a], w_a.at[yi])
    load_wb = load(weight_h.at[:, cols_b], w_b.at[xi])

    load_states.wait()
    packed = st_v[...].reshape(2, nr, piece, STATE)
    for b in range(2):
        send1[:, b * piece : (b + 1) * piece, :] = packed[b].astype(BF16)
    load_tx.wait()
    load_tb.wait()
    load_tc.wait()
    for row in range(TAIL_ROWS):
        t, part = row // 4, row % 4
        for b in range(2):
            src = tailx_v if part < 2 else tailbc_v
            lanes = slice((part % 2) * STATE, (part % 2 + 1) * STATE)
            at = b * tail_p + row % tail_p
            tsend1[row // tail_p, at : at + 1, :] = src[b, t : t + 1, lanes]

    load_dt.wait()
    head_lane = iota((1, heads), 1)
    bias_row = jnp.zeros((1, heads), F32)
    rate_row = jnp.zeros((1, heads), F32)
    skip_row = jnp.zeros((1, heads), F32)
    for h in range(heads):
        bias_row = jnp.where(head_lane == h, bias_s[h], bias_row)
        rate_row = jnp.where(head_lane == h, rates_s[h], rate_row)
        skip_row = jnp.where(head_lane == h, skip_s[h], skip_row)
    spread = (iota((heads, width), 1) // HEAD_DIM == iota((heads, width), 0)).astype(F32)
    eye_h = (iota((heads, heads), 0) == iota((heads, heads), 1)).astype(F32)
    row_i = iota((slot, slot), 0)
    col_i = iota((slot, slot), 1)
    causal = row_i >= col_i
    lower = causal.astype(F32)

    for q in range(2):
        raw = dt_v[q * slot : (q + 1) * slot, :] + bias_row
        soft = jnp.maximum(raw, 0.0) + jnp.log1p(jnp.exp(-jnp.abs(raw)))
        live = iota((slot, heads), 0) < lengths_s[q]
        dt = jnp.where(live, soft, 0.0)
        logdec = -dt * rate_row
        cum = jnp.dot(lower, logdec, precision=HIGHEST, preferred_element_type=F32)
        cum_t = dot_nt(eye_h, cum, HIGHEST)
        dt_t = dot_nt(eye_h, dt, HIGHEST)
        for h in range(heads):
            differ = cum[:, h : h + 1] - cum_t[h : h + 1, :]
            value = jnp.where(causal, jnp.exp(jnp.minimum(differ, 0.0)), 0.0)
            decay[q, h] = value * dt_t[h : h + 1, :]
        expcum[q] = jnp.dot(jnp.exp(cum), spread, precision=HIGHEST, preferred_element_type=F32)
        last = cum[slot - 1 : slot, :]
        weigh = jnp.exp(last - cum) * dt
        weighin[q] = jnp.dot(weigh, spread, precision=HIGHEST, preferred_element_type=F32)
        end_t = jnp.broadcast_to(jnp.exp(cum_t[:, slot - 1 : slot]), (heads, STATE))
        ending[q] = dot_tn(spread, end_t, HIGHEST)
    skip_wide = jnp.dot(skip_row, spread, precision=HIGHEST, preferred_element_type=F32)

    def raw_conv(seq, taps):
        total = seq * taps[3:4, :]
        at = iota(seq.shape, 0)
        for n in range(1, 4):
            moved = jnp.where(at >= n, pltpu.roll(seq, n, 0), 0.0)
            total = total + moved * taps[3 - n : 4 - n, :]
        return total

    load_x.wait()
    load_cx.wait()
    load_b.wait()
    load_c.wait()
    load_cb.wait()
    load_cc.wait()
    load_z.wait()
    for q in range(2):
        part = slice(q * slot, (q + 1) * slot)
        xraw[q] = raw_conv(x_v[part, :].astype(F32), convx_v[...])
        bcraw[q] = raw_conv(bc_v[part, :].astype(F32), convbc_v[...])
        gate[q] = silu(z_v[part, :].astype(F32))
    load_g.wait()
    load_wa.wait()
    load_wb.wait()

    pl.semaphore_wait(barrier, expected)

    def first_copy(rr):
        return remote(send1.at[rr], recv1.at[me_r], s1_send.at[rr], s1_recv.at[me_r], rr, me_t)

    def first_tail(rr):
        return remote(tsend1.at[rr], trecv1.at[me_r], t1_send.at[rr], t1_recv.at[me_r], rr, me_t)

    def start_first(rr):
        first_copy(rr).start()

        @pl.when(rr < tail_n)
        def _():
            first_tail(rr).start()

    each_replica(start_first)
    own1 = pltpu.make_async_copy(send1.at[me_r], recv1.at[me_r], own_sem.at[0])
    own1.start()

    @pl.when(me_r < tail_n)
    def _():
        copy = pltpu.make_async_copy(tsend1.at[me_r], trecv1.at[me_r], own_sem.at[1])
        copy.start()
        copy.wait()

    up_y, dn_y = (yi + 1) % ny, (yi + ny - 1) % ny
    up_x, dn_x = (xi + 1) % nx, (xi + nx - 1) % nx
    fill = w_a.shape[1] // 2

    def weight_copy(buf, at, lo, size, index, tt):
        ref = buf.at[at, pl.ds(lo, size), :]
        return remote(ref, ref, w_send.at[index], w_recv.at[index], me_r, tt)

    whole = 2 * fill
    wa_up = weight_copy(w_a, yi, 0, whole, 0, tensor_of(xi, up_y))
    wb_up = weight_copy(w_b, xi, 0, whole, 2, tensor_of(up_x, yi))
    wa_up.start()
    wb_up.start()
    if ny > 2:
        wa_dn = weight_copy(w_a, yi, 0, whole, 1, tensor_of(xi, dn_y))
        wa_dn.start()
    if nx > 2:
        wb_dn = weight_copy(w_b, xi, 0, whole, 3, tensor_of(dn_x, yi))
        wb_dn.start()

    def wait_first(rr):
        remote(send1.at[rr], recv1.at[rr], s1_send.at[rr], s1_recv.at[rr], rr, me_t).wait_recv()

        @pl.when(me_r < tail_n)
        def _():
            remote(
                tsend1.at[0], trecv1.at[rr], t1_send.at[0], t1_recv.at[rr], rr, me_t
            ).wait_recv()

    own1.wait()
    each_replica(wait_first)

    def pick(block):
        both = recv1[block // 2].astype(F32)
        return jnp.where(block % 2 == 1, both[piece:, :], both[:piece, :])

    def choose(rr, carry):
        first = pick(prefix_s[2 * rr])
        second = pick(prefix_s[2 * rr + 1])
        send2[rr] = jnp.concatenate([first, second], axis=0).astype(BF16)
        return carry

    lax.fori_loop(0, nr, choose, 0)

    @pl.when(me_r < tail_n)
    def _():
        def choose_tail(rr, carry):
            for s in range(2):
                block = prefix_s[2 * rr + s]
                both = trecv1[block // 2]
                tsend2[rr, s * tail_p : (s + 1) * tail_p, :] = jnp.where(
                    block % 2 == 1, both[tail_p:, :], both[:tail_p, :]
                )
            return carry

        lax.fori_loop(0, nr, choose_tail, 0)

    def start_second(rr):
        remote(
            send2.at[rr], recv2.at[me_r], s2_send.at[rr], s2_recv.at[me_r], rr, me_t
        ).start()

        @pl.when(me_r < tail_n)
        def _():
            remote(
                tsend2.at[rr], trecv2.at[me_r], t2_send.at[rr], t2_recv.at[me_r], rr, me_t
            ).start()

    each_replica(start_second)
    own2 = pltpu.make_async_copy(send2.at[me_r], recv2.at[me_r], own_sem.at[2])
    own2.start()

    @pl.when(me_r < tail_n)
    def _():
        copy = pltpu.make_async_copy(tsend2.at[me_r], trecv2.at[me_r], own_sem.at[3])
        copy.start()
        copy.wait()

    def weight_wait(buf, at, lo, size, index):
        weight_copy(buf, at, lo, size, index, me_t).wait_recv()

    weight_wait(w_a, dn_y, 0, whole, 0)
    weight_wait(w_b, dn_x, 0, whole, 2)
    forwards = []
    if ny > 2:
        weight_wait(w_a, up_y, 0, whole, 1)
        forwards.append(weight_copy(w_a, dn_y, 0, fill, 4, tensor_of(xi, up_y)))
        forwards.append(weight_copy(w_a, up_y, fill, fill, 5, tensor_of(xi, dn_y)))
    if nx > 2:
        weight_wait(w_b, up_x, 0, whole, 3)
        forwards.append(weight_copy(w_b, dn_x, 0, fill, 6, tensor_of(up_x, yi)))
        forwards.append(weight_copy(w_b, up_x, fill, fill, 7, tensor_of(dn_x, yi)))
    for copy in forwards:
        copy.start()

    def wait_second(rr):
        remote(send2.at[rr], recv2.at[rr], s2_send.at[rr], s2_recv.at[rr], rr, me_t).wait_recv()

        @pl.when(rr < tail_n)
        def _():
            remote(
                tsend2.at[0], trecv2.at[rr], t2_send.at[0], t2_recv.at[rr], rr, me_t
            ).wait_recv()

    own2.wait()
    each_replica(wait_second)

    lane_head = iota((1, width), 1) // HEAD_DIM
    saved = []
    for q in range(2):
        start_at = recv2[...].astype(F32)[:, q * piece : (q + 1) * piece, :]
        start_at = start_at.reshape(width, STATE)
        at8 = iota((8, STATE), 0)

        def tail_tile(part):
            tile = jnp.zeros((8, STATE), F32)
            for t in range(3):
                row = t * 4 + part
                at = q * tail_p + row % tail_p
                line = trecv2[row // tail_p, at : at + 1, :]
                tile = jnp.where(at8 == t, line, tile)
            return tile

        def tail_fix(tile, taps):
            total = tile * taps[0:1, :]
            rolled = jnp.where(at8 < 3, pltpu.roll(tile, 7, 0), 0.0)
            total = total + rolled * taps[1:2, :]
            rolled = jnp.where(at8 < 3, pltpu.roll(tile, 6, 0), 0.0)
            return total + rolled * taps[2:3, :]

        for part in range(2):
            lanes = slice(part * STATE, (part + 1) * STATE)
            xraw[q, 0:8, lanes] += tail_fix(tail_tile(part), convx_v[:, lanes])
            bcraw[q, 0:8, lanes] += tail_fix(tail_tile(part + 2), convbc_v[:, lanes])
        xc = silu(xraw[q])
        bcc = silu(bcraw[q])
        b_low = bcc[:, :STATE].astype(BF16)
        c_low = bcc[:, STATE:].astype(BF16)
        scores = dot_nt(c_low, b_low)
        y = expcum[q] * dot_nt(c_low, start_at.astype(BF16)) + skip_wide * xc
        for hp in range(heads // 2):
            left, right = 2 * hp, 2 * hp + 1
            mixing = jnp.concatenate([scores * decay[q, left], scores * decay[q, right]], axis=1)
            held = jnp.concatenate(
                [jnp.where(lane_head == left, xc, 0.0), jnp.where(lane_head == right, xc, 0.0)],
                axis=0,
            )
            y = y + jnp.dot(mixing.astype(BF16), held.astype(BF16), preferred_element_type=F32)
        v = y * gate[q]
        ss_send[:, q * slot : (q + 1) * slot] = dot_nt(jnp.ones((8, width), F32), v * v, HIGHEST)
        live = iota((slot, width), 0) < lengths_s[q]
        v = jnp.where(live, v * gain_v[...], 0.0)
        v_f[q] = v
        owners = slot // rows_owner // ny
        v_a[q * owners : (q + 1) * owners] = v.astype(BF16).reshape(owners, ny, rows_owner, width)
        saved.append((start_at, xc, b_low))

    def ss_copy(yy, cc):
        return remote(
            ss_send,
            ss_recv.at[ci, yi],
            ss_ssem.at[cc, yy],
            ss_rsem.at[ci, yi],
            zi * 2 + cc,
            tensor_of(xi, yy),
        )

    def va_copy(yy, cc):
        return remote(
            v_a.at[:, yy],
            r_a.at[ci, yi],
            va_send.at[cc, yy],
            va_recv.at[ci, yi],
            zi * 2 + cc,
            tensor_of(xi, yy),
        )

    for yy, cc in y_peers():
        ss_copy(yy, cc).start()
    for yy, cc in y_peers():
        va_copy(yy, cc).start()
    ss_recv[ci, yi] = ss_send[...]
    own_a = pltpu.make_async_copy(v_a.at[:, yi], r_a.at[ci, yi], own_sem.at[4])
    own_a.start()

    for q in range(2):
        start_at, xc, b_low = saved[q]
        weighed = (xc * weighin[q]).astype(BF16)
        final_o[q] = ending[q] * start_at + dot_tn(weighed, b_low)

    def ss_wait(yy, cc):
        remote(
            ss_send,
            ss_recv.at[cc, yy],
            ss_ssem.at[cc, yy],
            ss_rsem.at[cc, yy],
            zi * 2 + cc,
            tensor_of(xi, yy),
        ).wait_recv()

    for yy, cc in y_peers():
        ss_wait(yy, cc)
    scale_t = []
    for cc in range(2):
        total = ss_recv[cc, 0]
        for yy in range(1, ny):
            total = total + ss_recv[cc, yy]
        scale_t.append(lax.rsqrt(total / (ny * width) + EPSILON))
    mine = jnp.where(ci == 0, scale_t[0], scale_t[1])
    eye_t = (iota((tokens, tokens), 0) == iota((tokens, tokens), 1)).astype(F32)
    column = dot_nt(eye_t, mine, HIGHEST)
    for q in range(2):
        scaled = v_f[q] * column[q * slot : (q + 1) * slot, 0:1]
        v_b[q * owners : (q + 1) * owners] = scaled.astype(BF16).reshape(
            owners, ny, rows_owner, width
        )

    def vb_copy(xx, cc):
        return remote(
            v_b.at[xx],
            r_b.at[ci, xi],
            vb_send.at[cc, xx],
            vb_recv.at[ci, xi],
            zi * 2 + cc,
            tensor_of(xx, yi),
        )

    for xx, cc in x_peers():
        vb_copy(xx, cc).start()
    own_b = pltpu.make_async_copy(v_b.at[xi], r_b.at[ci, xi], own_sem.at[5])
    own_b.start()

    if ny > 2:
        opp_y = (yi + 2) % ny
        weight_wait(w_a, opp_y, 0, fill, 4)
        weight_wait(w_a, opp_y, fill, fill, 5)
    for yy, cc in y_peers():
        remote(
            v_a.at[:, yi],
            r_a.at[cc, yy],
            va_send.at[cc, yy],
            va_recv.at[cc, yy],
            zi * 2 + cc,
            tensor_of(xi, yy),
        ).wait_recv()
    own_a.wait()
    rows_a = 2 * nx * rows_owner
    acc = jnp.zeros((rows_a, quarter), F32)
    for yy in range(ny):
        lhs = r_a[:, yy].reshape(rows_a, width)
        acc = acc + jnp.dot(lhs, w_a[yy], preferred_element_type=F32)
    per = nx * rows_owner
    where_row = iota((per, tokens), 0)
    wanted = (where_row // rows_owner * ny + yi) * rows_owner + where_row % rows_owner
    pick_rows = (iota((per, tokens), 1) == wanted).astype(F32)
    for cc in range(2):
        col = dot_nt(pick_rows, scale_t[cc], HIGHEST)[:, 0:1]
        part = acc[cc * per : (cc + 1) * per, :] * col
        o_a[cc] = part.astype(BF16).reshape(nx, rows_owner, quarter)

    for xx, cc in x_peers():
        remote(
            o_a.at[cc, xx],
            ro_a.at[xi, ci],
            oa_send.at[xx, cc],
            oa_recv.at[xi, ci],
            zi * 2 + cc,
            tensor_of(xx, yi),
        ).start()
    own_oa = pltpu.make_async_copy(o_a.at[ci, xi], ro_a.at[xi, ci], own_sem.at[6])
    own_oa.start()

    if nx > 2:
        opp_x = (xi + 2) % nx
        weight_wait(w_b, opp_x, 0, fill, 6)
        weight_wait(w_b, opp_x, fill, fill, 7)
    for xx, cc in x_peers():
        remote(
            v_b.at[xi],
            r_b.at[cc, xx],
            vb_send.at[cc, xx],
            vb_recv.at[cc, xx],
            zi * 2 + cc,
            tensor_of(xx, yi),
        ).wait_recv()
    own_b.wait()
    rows_b = 2 * ny * rows_owner
    acc = jnp.zeros((rows_b, quarter), F32)
    for xx in range(nx):
        lhs = r_b[:, xx].reshape(rows_b, width)
        acc = acc + jnp.dot(lhs, w_b[xx], preferred_element_type=F32)
    o_b[...] = acc.astype(BF16).reshape(2, ny, rows_owner, quarter)
    for yy, cc in y_peers():
        remote(
            o_b.at[cc, yy],
            ro_b.at[yi, ci],
            ob_send.at[yy, cc],
            ob_recv.at[yi, ci],
            zi * 2 + cc,
            tensor_of(xi, yy),
        ).start()
    own_ob = pltpu.make_async_copy(o_b.at[ci, yi], ro_b.at[yi, ci], own_sem.at[7])
    own_ob.start()

    for xx, cc in x_peers():
        remote(
            o_a.at[cc, xx],
            ro_a.at[xx, cc],
            oa_send.at[xx, cc],
            oa_recv.at[xx, cc],
            zi * 2 + cc,
            tensor_of(xx, yi),
        ).wait_recv()
    own_oa.wait()
    for cc in range(2):
        total = ro_a[0, cc].astype(F32)
        for xx in range(1, nx):
            total = total + ro_a[xx, cc].astype(F32)
        mixed_o[:, cc * quarter : (cc + 1) * quarter] = total.astype(BF16)
    for yy, cc in y_peers():
        remote(
            o_b.at[cc, yy],
            ro_b.at[yy, cc],
            ob_send.at[yy, cc],
            ob_recv.at[yy, cc],
            zi * 2 + cc,
            tensor_of(xi, yy),
        ).wait_recv()
    own_ob.wait()
    for cc in range(2):
        total = ro_b[0, cc].astype(F32)
        for yy in range(1, ny):
            total = total + ro_b[yy, cc].astype(F32)
        lo = half_cols + cc * quarter
        mixed_o[:, lo : lo + quarter] = total.astype(BF16)

    def sent(rr):
        first_copy(rr).wait_send()
        remote(
            send2.at[rr], recv2.at[me_r], s2_send.at[rr], s2_recv.at[me_r], rr, me_t
        ).wait_send()

        @pl.when(rr < tail_n)
        def _():
            first_tail(rr).wait_send()

        @pl.when(me_r < tail_n)
        def _():
            remote(
                tsend2.at[rr], trecv2.at[me_r], t2_send.at[rr], t2_recv.at[me_r], rr, me_t
            ).wait_send()

    each_replica(sent)
    wa_up.wait_send()
    wb_up.wait_send()
    if ny > 2:
        wa_dn.wait_send()
    if nx > 2:
        wb_dn.wait_send()
    for copy in forwards:
        copy.wait_send()
    for yy, cc in y_peers():
        ss_copy(yy, cc).wait_send()
        va_copy(yy, cc).wait_send()
        remote(
            o_b.at[cc, yy],
            ro_b.at[yi, ci],
            ob_send.at[yy, cc],
            ob_recv.at[yi, ci],
            zi * 2 + cc,
            tensor_of(xi, yy),
        ).wait_send()
    for xx, cc in x_peers():
        vb_copy(xx, cc).wait_send()
        remote(
            o_a.at[cc, xx],
            ro_a.at[xi, ci],
            oa_send.at[xx, cc],
            oa_recv.at[xi, ci],
            zi * 2 + cc,
            tensor_of(xx, yi),
        ).wait_send()


def local(
    sizes,
    x_input,
    z_input,
    bc_input,
    dt_raw,
    dt_bias,
    decay_rates,
    skip_gain,
    conv_x,
    conv_bc,
    norm_gain,
    out_weight,
    cached_states,
    cached_tail_x,
    cached_tail_bc,
    prefix_block,
    lengths,
):
    nr, nx, ny = sizes
    tokens, width = x_input.shape
    heads = dt_raw.shape[1]
    slot = tokens // 2
    out_cols = out_weight.shape[1]
    quarter = out_cols // 4
    rows_owner = tokens // (nx * ny)
    piece = width // nr
    tail_n = min(nr, TAIL_ROWS)
    tail_p = TAIL_ROWS // tail_n
    vmem = pltpu.VMEM
    dma = pltpu.SemaphoreType.DMA
    smem_spec = pl.BlockSpec(memory_space=pltpu.SMEM)
    any_spec = pl.BlockSpec(memory_space=pl.ANY)
    vmem_spec = pl.BlockSpec(memory_space=pltpu.VMEM)
    scratch = [
        vmem((tokens, width), BF16),
        vmem((tokens, width), BF16),
        vmem((tokens, 2 * STATE), BF16),
        vmem((tokens, heads), F32),
        vmem((4, width), F32),
        vmem((4, 2 * STATE), F32),
        vmem((1, width), F32),
        vmem((2, width, STATE), F32),
        vmem((2, 3, width), F32),
        vmem((2, 3, 2 * STATE), F32),
        vmem((nr, 2 * piece, STATE), BF16),
        vmem((nr, 2 * piece, STATE), BF16),
        vmem((nr, 2 * piece, STATE), BF16),
        vmem((nr, 2 * piece, STATE), BF16),
        vmem((tail_n, 2 * tail_p, STATE), F32),
        vmem((nr, 2 * tail_p, STATE), F32),
        vmem((nr, 2 * tail_p, STATE), F32),
        vmem((tail_n, 2 * tail_p, STATE), F32),
        vmem((ny, width, quarter), BF16),
        vmem((nx, width, quarter), BF16),
        vmem((2, slot, width), F32),
        vmem((2, slot, 2 * STATE), F32),
        vmem((2, slot, width), F32),
        vmem((2, heads, slot, slot), F32),
        vmem((2, slot, width), F32),
        vmem((2, slot, width), F32),
        vmem((2, width, STATE), F32),
        vmem((2, slot, width), F32),
        vmem((nx, ny, rows_owner, width), BF16),
        vmem((nx, ny, rows_owner, width), BF16),
        vmem((2, ny, nx, rows_owner, width), BF16),
        vmem((2, nx, ny, rows_owner, width), BF16),
        vmem((8, tokens), F32),
        vmem((2, ny, 8, tokens), F32),
        vmem((2, nx, rows_owner, quarter), BF16),
        vmem((2, ny, rows_owner, quarter), BF16),
        vmem((nx, 2, rows_owner, quarter), BF16),
        vmem((ny, 2, rows_owner, quarter), BF16),
        dma((15,)),
        dma((8,)),
        dma((nr,)),
        dma((nr,)),
        dma((nr,)),
        dma((nr,)),
        dma((nr,)),
        dma((nr,)),
        dma((nr,)),
        dma((nr,)),
        dma((8,)),
        dma((8,)),
        dma((2, ny)),
        dma((2, ny)),
        dma((2, nx)),
        dma((2, nx)),
        dma((2, ny)),
        dma((2, ny)),
        dma((nx, 2)),
        dma((nx, 2)),
        dma((ny, 2)),
        dma((ny, 2)),
    ]
    mixed, final_states = pl.pallas_call(
        functools.partial(layer_kernel, sizes),
        out_shape=(
            jax.ShapeDtypeStruct((rows_owner, out_cols), BF16),
            jax.ShapeDtypeStruct((2, width, STATE), F32),
        ),
        in_specs=[smem_spec] * 5 + [any_spec] * 11,
        out_specs=(vmem_spec, vmem_spec),
        scratch_shapes=scratch,
        compiler_params=pltpu.CompilerParams(
            collective_id=0, has_side_effects=True, vmem_limit_bytes=56 * 1024 * 1024
        ),
        name="prefill_layer",
    )(
        prefix_block,
        lengths,
        dt_bias,
        decay_rates,
        skip_gain,
        x_input,
        z_input,
        bc_input,
        dt_raw,
        conv_x,
        conv_bc,
        norm_gain.reshape(1, width),
        out_weight,
        cached_states.reshape(2, width, STATE),
        cached_tail_x,
        cached_tail_bc,
    )
    return mixed, final_states.reshape(2, heads, HEAD_DIM, STATE)


def tensor_grid(count):
    side = 1
    while side * side < count:
        side *= 2
    return side, count // side


def solution(mesh):
    placed = (
        P("replica", "tensor"),
        P("replica", "tensor"),
        P("replica", None),
        P("replica", "tensor"),
        P("tensor"),
        P("tensor"),
        P("tensor"),
        P(None, "tensor"),
        P(),
        P("tensor"),
        P("tensor", None),
        P("replica", "tensor", None, None),
        P("replica", None, "tensor"),
        P("replica", None, None),
        P(),
        P("replica"),
    )
    sizes = (mesh.shape["replica"],) + tensor_grid(mesh.shape["tensor"])
    return jax.shard_map(
        functools.partial(local, sizes),
        mesh=mesh,
        in_specs=placed,
        out_specs=(P(("replica", "tensor"), None), P("replica", "tensor", None, None)),
        check_vma=False,
    )
```

time: 262 us -> 68.1 us (0.26)
  blocking collectives: 101 us -> 0 us
  waiting for transfers between devices: 83.2 us -> 0 us
  Pallas kernels: 0 us -> 59.7 us
  other arithmetic: 21.4 us -> 0 us
  matrix products: 18.7 us -> 0 us
  local copies, waits for them, and re-layouts: 22.3 us -> 7.37 us
  between operations: 14.5 us -> 0.64 us
    reduce_scatter x1 -> x0, waiting for transfers between devices: 83.2 us -> none  [local(): lax.psum_scatter(jnp.dot(gated, out_weight, preferred_element_type=jnp.fl...]
    all_gather x2 -> x0, blocking collectives: 66.7 us -> none  [the longest x1 39.2 us: local(): lax.all_gather(cached_tail_bc.astype(jnp.bfloat16), 'replica', axis=0, ti...]
    pallas_call x0 -> x1, Pallas kernels: none -> 59.7 us  [local(): pl.pallas_call(functools.partial(layer_kernel, sizes), out_shape=(jax.Sha...]
    psum x1 -> x0, blocking collectives: 34 us -> none  [local(): totals = lax.psum(partial_sq, 'tensor')]
    dot_general x15 -> x0, matrix products: 18.7 us -> none  [the longest x2 4.12 us: span_scan(): jnp.einsum('ihn,hpn->ihp', c_heads, carry_state, precision=highest)]
    convert_element_type x9 -> x0, other arithmetic: 13.1 us -> none  [the longest x1 6.65 us: local(): lax.all_gather(cached_states.astype(jnp.bfloat16), 'replica', axis=0, til...]
    gather x3 -> x0, local copies, waits for them, and re-layouts: 6.99 us -> none  [local(): taken_rows = jnp.take(piece, position, axis=0)]
    exp x6 -> x0, local copies, waits for them, and re-layouts: 5.67 us -> none  [the longest x4 4.3 us: span_scan(): jnp.exp(cumulative)[:, :, None]]
  transfers between devices with their start and end apart: 2 -> 0, of which waited for: 1 -> 0; matrix products, arithmetic and copies ran while one was open for 15% -> 0% of each run, Pallas kernels for 0% -> 0%
where the time goes in v1:
time: 68.1 us; the launch traced here: 67.7 us
  Pallas kernels  59.7 us (88%)
  local copies, waits for them, and re-layouts  7.37 us (11%)
    pallas_call x1, Pallas kernels, local(): pl.pallas_call(functools.partial(layer_kernel, sizes), out_shape=(jax.Sha...  59.7 us
    unnamed x5, local copies, waits for them, and re-layouts  7.37 us

profile of v1, /device:TPU:1, one launch (start us, length us, event | category | flops | bytes accessed | tf_op | source)
XLA Modules:
  0.0 67.7 jit_solution(2890249164870653743)
XLA Ops:
  0.6 1.3 %copy.19.tailx_h = f32[2,3,256]{2,1,0:T(4,128)} copy(f32[2,3,256]{2,0,1:T(2,128)} %param.28) | data formatting | bytes 12288 | tf_op args[12]
  1.9 1.4 %copy.20.tailbc_h = f32[2,3,1024]{2,1,0:T(4,128)} copy(f32[2,3,1024]{2,0,1:T(2,128)} %param.29) | data formatting | bytes 49152 | tf_op args[13]
  3.3 1.5 %copy.18.dt_h = f32[256,8]{1,0:T(8,128)} copy(f32[256,8]{0,1:T(8,128)} %param.19) | data formatting | bytes 16384 | tf_op args[3]
  4.8 59.7 %prefill_layer.1 = (bf16[16,4096]{1,0:T(8,128)(2,1)}, f32[2,256,128]{2,1,0:T(8,128)}) custom-call(s32[64]{0:T(128)} %prefix_s.1, s32[2]{0:T(128)} %lengths_s.1, f32[8]{0:T(128)} %bias_s.1, f32[8]{0:T(128)} %rates_s.1, f32[8]{0:T(128)} %skip_s.1, bf16[256,256]{1,0:T(8,128)(2,1)} %x_h.1, bf16[256,256]{1,0:T(8,128)(2,1)} %z_h.1, bf16[256,1024]{1,0:T(8,128)(2,1)} %bc_h.1, ...), custom_call_target="tpu_custom_call" | custom-call | tf_op jit(solution)/shard_map/prefill_layer/pallas_call | solution.py:803
  64.5 1.6 %copy.23 = bf16[16,4096]{1,0:T(8,128)(2,1)} copy(bf16[16,4096]{1,0:T(8,128)(2,1)} %get-tuple-element.8) | data formatting | bytes 262144
  66.0 1.7 %copy.24 = f32[2,8,32,128]{3,2,1,0:T(8,128)} copy(f32[2,8,32,128]{3,2,1,0:T(8,128)} %bitcast.4) | data formatting | bytes 524288

commit v2 on v1

--- a/solution.py
+++ b/solution.py
@@ -232,43 +232,87 @@
             src = tailx_v if part < 2 else tailbc_v
             lanes = slice((part % 2) * STATE, (part % 2 + 1) * STATE)
             at = b * tail_p + row % tail_p
-            tsend1[row // tail_p, at : at + 1, :] = src[b, t : t + 1, lanes]
+            tsend1[row // tail_p, at : at + 1, :] = src[t, b : b + 1, lanes]
+
+    pl.semaphore_wait(barrier, expected)
+
+    def first_copy(rr):
+        return remote(send1.at[rr], recv1.at[me_r], s1_send.at[rr], s1_recv.at[me_r], rr, me_t)
+
+    def first_tail(rr):
+        return remote(tsend1.at[rr], trecv1.at[me_r], t1_send.at[rr], t1_recv.at[me_r], rr, me_t)
+
+    def start_first(rr):
+        first_copy(rr).start()
+
+        @pl.when(rr < tail_n)
+        def _():
+            first_tail(rr).start()
+
+    each_replica(start_first)
+    own1 = pltpu.make_async_copy(send1.at[me_r], recv1.at[me_r], own_sem.at[0])
+    own1.start()
+
+    @pl.when(me_r < tail_n)
+    def _():
+        copy = pltpu.make_async_copy(tsend1.at[me_r], trecv1.at[me_r], own_sem.at[1])
+        copy.start()
+        copy.wait()
+
+    up_y, dn_y = (yi + 1) % ny, (yi + ny - 1) % ny
+    up_x, dn_x = (xi + 1) % nx, (xi + nx - 1) % nx
+    fill = w_a.shape[1] // 2
+
+    def weight_copy(buf, at, lo, size, index, tt):
+        ref = buf.at[at, pl.ds(lo, size), :]
+        return remote(ref, ref, w_send.at[index], w_recv.at[index], me_r, tt)
+
+    whole = 2 * fill
+    load_wa.wait()
+    load_wb.wait()
+    wa_up = weight_copy(w_a, yi, 0, whole, 0, tensor_of(xi, up_y))
+    wb_up = weight_copy(w_b, xi, 0, whole, 2, tensor_of(up_x, yi))
+    wa_up.start()
+    wb_up.start()
+    if ny > 2:
+        wa_dn = weight_copy(w_a, yi, 0, whole, 1, tensor_of(xi, dn_y))
+        wa_dn.start()
+    if nx > 2:
+        wb_dn = weight_copy(w_b, xi, 0, whole, 3, tensor_of(dn_x, yi))
+        wb_dn.start()
 
     load_dt.wait()
+    head_row = iota((heads, 1), 0)
     head_lane = iota((1, heads), 1)
-    bias_row = jnp.zeros((1, heads), F32)
-    rate_row = jnp.zeros((1, heads), F32)
+    bias_col = jnp.zeros((heads, 1), F32)
+    rate_col = jnp.zeros((heads, 1), F32)
     skip_row = jnp.zeros((1, heads), F32)
     for h in range(heads):
-        bias_row = jnp.where(head_lane == h, bias_s[h], bias_row)
-        rate_row = jnp.where(head_lane == h, rates_s[h], rate_row)
+        bias_col = jnp.where(head_row == h, bias_s[h], bias_col)
+        rate_col = jnp.where(head_row == h, rates_s[h], rate_col)
         skip_row = jnp.where(head_lane == h, skip_s[h], skip_row)
     spread = (iota((heads, width), 1) // HEAD_DIM == iota((heads, width), 0)).astype(F32)
-    eye_h = (iota((heads, heads), 0) == iota((heads, heads), 1)).astype(F32)
     row_i = iota((slot, slot), 0)
     col_i = iota((slot, slot), 1)
     causal = row_i >= col_i
     lower = causal.astype(F32)
 
     for q in range(2):
-        raw = dt_v[q * slot : (q + 1) * slot, :] + bias_row
+        raw = dt_v[:, q * slot : (q + 1) * slot] + bias_col
         soft = jnp.maximum(raw, 0.0) + jnp.log1p(jnp.exp(-jnp.abs(raw)))
-        live = iota((slot, heads), 0) < lengths_s[q]
-        dt = jnp.where(live, soft, 0.0)
-        logdec = -dt * rate_row
-        cum = jnp.dot(lower, logdec, precision=HIGHEST, preferred_element_type=F32)
-        cum_t = dot_nt(eye_h, cum, HIGHEST)
-        dt_t = dot_nt(eye_h, dt, HIGHEST)
+        live = iota((heads, slot), 1) < lengths_s[q]
+        dt_t = jnp.where(live, soft, 0.0)
+        logdec = -dt_t * rate_col
+        cum = dot_nt(lower, logdec, HIGHEST)
+        cum_t = dot_nt(logdec, lower, HIGHEST)
         for h in range(heads):
             differ = cum[:, h : h + 1] - cum_t[h : h + 1, :]
             value = jnp.where(causal, jnp.exp(jnp.minimum(differ, 0.0)), 0.0)
             decay[q, h] = value * dt_t[h : h + 1, :]
-        expcum[q] = jnp.dot(jnp.exp(cum), spread, precision=HIGHEST, preferred_element_type=F32)
-        last = cum[slot - 1 : slot, :]
-        weigh = jnp.exp(last - cum) * dt
-        weighin[q] = jnp.dot(weigh, spread, precision=HIGHEST, preferred_element_type=F32)
-        end_t = jnp.broadcast_to(jnp.exp(cum_t[:, slot - 1 : slot]), (heads, STATE))
-        ending[q] = dot_tn(spread, end_t, HIGHEST)
+        expcum[q] = dot_tn(jnp.exp(cum_t), spread, HIGHEST)
+        last = cum_t[:, slot - 1 : slot]
+        weighin[q] = dot_tn(jnp.exp(last - cum_t) * dt_t, spread, HIGHEST)
+        ending[q] = dot_tn(spread, jnp.broadcast_to(jnp.exp(last), (heads, STATE)), HIGHEST)
     skip_wide = jnp.dot(skip_row, spread, precision=HIGHEST, preferred_element_type=F32)
 
     def raw_conv(seq, taps):
@@ -292,53 +336,6 @@
         bcraw[q] = raw_conv(bc_v[part, :].astype(F32), convbc_v[...])
         gate[q] = silu(z_v[part, :].astype(F32))
     load_g.wait()
-    load_wa.wait()
-    load_wb.wait()
-
-    pl.semaphore_wait(barrier, expected)
-
-    def first_copy(rr):
-        return remote(send1.at[rr], recv1.at[me_r], s1_send.at[rr], s1_recv.at[me_r], rr, me_t)
-
-    def first_tail(rr):
-        return remote(tsend1.at[rr], trecv1.at[me_r], t1_send.at[rr], t1_recv.at[me_r], rr, me_t)
-
-    def start_first(rr):
-        first_copy(rr).start()
-
-        @pl.when(rr < tail_n)
-        def _():
-            first_tail(rr).start()
-
-    each_replica(start_first)
-    own1 = pltpu.make_async_copy(send1.at[me_r], recv1.at[me_r], own_sem.at[0])
-    own1.start()
-
-    @pl.when(me_r < tail_n)
-    def _():
-        copy = pltpu.make_async_copy(tsend1.at[me_r], trecv1.at[me_r], own_sem.at[1])
-        copy.start()
-        copy.wait()
-
-    up_y, dn_y = (yi + 1) % ny, (yi + ny - 1) % ny
-    up_x, dn_x = (xi + 1) % nx, (xi + nx - 1) % nx
-    fill = w_a.shape[1] // 2
-
-    def weight_copy(buf, at, lo, size, index, tt):
-        ref = buf.at[at, pl.ds(lo, size), :]
-        return remote(ref, ref, w_send.at[index], w_recv.at[index], me_r, tt)
-
-    whole = 2 * fill
-    wa_up = weight_copy(w_a, yi, 0, whole, 0, tensor_of(xi, up_y))
-    wb_up = weight_copy(w_b, xi, 0, whole, 2, tensor_of(up_x, yi))
-    wa_up.start()
-    wb_up.start()
-    if ny > 2:
-        wa_dn = weight_copy(w_a, yi, 0, whole, 1, tensor_of(xi, dn_y))
-        wa_dn.start()
-    if nx > 2:
-        wb_dn = weight_copy(w_b, xi, 0, whole, 3, tensor_of(dn_x, yi))
-        wb_dn.start()
 
     def wait_first(rr):
         remote(send1.at[rr], recv1.at[rr], s1_send.at[rr], s1_recv.at[rr], rr, me_t).wait_recv()
@@ -702,6 +699,15 @@
             zi * 2 + cc,
             tensor_of(xx, yi),
         ).wait_send()
+
+
+def store_kernel(mixed_v, final_v, mixed_o, final_o, sem):
+    first = pltpu.make_async_copy(mixed_v, mixed_o, sem.at[0])
+    second = pltpu.make_async_copy(final_v, final_o, sem.at[1])
+    first.start()
+    second.start()
+    first.wait()
+    second.wait()
 
 
 def local(
@@ -736,19 +742,19 @@
     vmem = pltpu.VMEM
     dma = pltpu.SemaphoreType.DMA
     smem_spec = pl.BlockSpec(memory_space=pltpu.SMEM)
-    any_spec = pl.BlockSpec(memory_space=pl.ANY)
+    hbm_spec = pl.BlockSpec(memory_space=pl.ANY)
     vmem_spec = pl.BlockSpec(memory_space=pltpu.VMEM)
     scratch = [
         vmem((tokens, width), BF16),
         vmem((tokens, width), BF16),
         vmem((tokens, 2 * STATE), BF16),
-        vmem((tokens, heads), F32),
+        vmem((heads, tokens), F32),
         vmem((4, width), F32),
         vmem((4, 2 * STATE), F32),
         vmem((1, width), F32),
         vmem((2, width, STATE), F32),
-        vmem((2, 3, width), F32),
-        vmem((2, 3, 2 * STATE), F32),
+        vmem((3, 2, width), F32),
+        vmem((3, 2, 2 * STATE), F32),
         vmem((nr, 2 * piece, STATE), BF16),
         vmem((nr, 2 * piece, STATE), BF16),
         vmem((nr, 2 * piece, STATE), BF16),
@@ -802,11 +808,8 @@
     ]
     mixed, final_states = pl.pallas_call(
         functools.partial(layer_kernel, sizes),
-        out_shape=(
-            jax.ShapeDtypeStruct((rows_owner, out_cols), BF16),
-            jax.ShapeDtypeStruct((2, width, STATE), F32),
-        ),
-        in_specs=[smem_spec] * 5 + [any_spec] * 11,
+        out_shape=(vmem((rows_owner, out_cols), BF16), vmem((2, width, STATE), F32)),
+        in_specs=[smem_spec] * 5 + [hbm_spec] * 11,
         out_specs=(vmem_spec, vmem_spec),
         scratch_shapes=scratch,
         compiler_params=pltpu.CompilerParams(
@@ -822,15 +825,27 @@
         x_input,
         z_input,
         bc_input,
-        dt_raw,
+        dt_raw.T,
         conv_x,
         conv_bc,
         norm_gain.reshape(1, width),
         out_weight,
         cached_states.reshape(2, width, STATE),
-        cached_tail_x,
-        cached_tail_bc,
+        jnp.transpose(cached_tail_x, (1, 0, 2)),
+        jnp.transpose(cached_tail_bc, (1, 0, 2)),
     )
+    mixed, final_states = pl.pallas_call(
+        store_kernel,
+        out_shape=(
+            jax.ShapeDtypeStruct((rows_owner, out_cols), BF16),
+            jax.ShapeDtypeStruct((2, width, STATE), F32),
+        ),
+        in_specs=[vmem_spec] * 2,
+        out_specs=(hbm_spec, hbm_spec),
+        scratch_shapes=[dma((2,))],
+        compiler_params=pltpu.CompilerParams(vmem_limit_bytes=4 * 1024 * 1024),
+        name="store_results",
+    )(mixed, final_states)
     return mixed, final_states.reshape(2, heads, HEAD_DIM, STATE)
 
 

time: 68.1 us -> 60.1 us (0.88)
  local copies, waits for them, and re-layouts: 7.37 us -> 0 us
    unnamed x5 -> x0, local copies, waits for them, and re-layouts: 7.37 us -> none
    pallas_call x1 -> x2, Pallas kernels: 59.7 us -> 59.3 us  [the longest x1 58.6 us: local(): pl.pallas_call(functools.partial(layer_kernel, sizes), out_shape=(vmem((r...]
where the time goes in v2:
time: 60.1 us; the launch traced here: 60 us
  Pallas kernels  59.3 us (99%)
  between operations  0.64 us (1%)
    pallas_call x1, Pallas kernels, local(): pl.pallas_call(functools.partial(layer_kernel, sizes), out_shape=(vmem((r...  58.6 us

profile of v2, /device:TPU:1, one launch (start us, length us, event | category | flops | bytes accessed | tf_op | source)
XLA Modules:
  0.0 60.0 jit_solution(5877935358039998436)
XLA Ops:
  0.6 58.6 %prefill_layer.1 = (bf16[16,4096]{1,0:T(8,128)(2,1)S(1)}, f32[2,256,128]{2,1,0:T(8,128)S(1)}) custom-call(s32[64]{0:T(128)} %prefix_s.1, s32[2]{0:T(128)} %lengths_s.1, f32[8]{0:T(128)} %bias_s.1, f32[8]{0:T(128)} %rates_s.1, f32[8]{0:T(128)} %skip_s.1, bf16[256,256]{1,0:T(8,128)(2,1)} %x_h.1, bf16[256,256]{1,0:T(8,128)(2,1)} %z_h.1, ...), custom_call_target="tpu_custom_call" | custom-call | tf_op jit(solution)/shard_map/prefill_layer/pallas_call | solution.py:809
  59.2 0.8 %store_results.1 = (bf16[16,4096]{1,0:T(8,128)(2,1)}, f32[2,256,128]{2,1,0:T(8,128)}) custom-call(bf16[16,4096]{1,0:T(8,128)(2,1)S(1)} %get-tuple-element.6.mixed_v, f32[2,256,128]{2,1,0:T(8,128)S(1)} %get-tuple-element.7.final_v), custom_call_target="tpu_custom_call" | custom-call | tf_op jit(solution)/shard_map/store_results/pallas_call | solution.py:837

commit v3 on v2

--- a/solution.py
+++ b/solution.py
@@ -83,9 +83,7 @@
     expcum,
     weighin,
     ending,
-    v_f,
     v_a,
-    v_b,
     r_a,
     r_b,
     ss_send,
@@ -135,13 +133,16 @@
     zi, ci = me_r // 2, me_r % 2
     xi, yi = me_t // ny, me_t % ny
 
+    def far_pair(m):
+        k = (m + 1) // 2
+        dz = nz // 2 + k * (1 - 2 * (m % 2))
+        return (zi + dz) % nz * 2
+
     def each_replica(fn):
         def step(m, carry):
-            k = (m + 1) // 2
-            dz = nz // 2 + k * (1 - 2 * (m % 2))
-            zz = (zi + dz) % nz
-            fn(zz * 2)
-            fn(zz * 2 + 1)
+            base = far_pair(m)
+            fn(base)
+            fn(base + 1)
             return carry
 
         lax.fori_loop(0, nz - 1, step, 0)
@@ -161,6 +162,15 @@
             for dc in range(2):
                 if d or dc:
                     out.append(((xi + d) % nx, (ci + dc) % 2))
+        return out
+
+    def grid_peers():
+        out = []
+        for dx in range(nx):
+            for dy in range(ny):
+                for cc in range(2):
+                    if dx or dy:
+                        out.append(((xi + dx) % nx, (yi + dy) % ny, cc))
         return out
 
     def tensor_of(xx, yy):
@@ -182,13 +192,9 @@
         pl.semaphore_signal(barrier, inc=1, device_id=(rr, tt), device_id_type=MESH)
 
     each_replica(lambda rr: greet(rr, me_t))
-    for d in range(1, ny):
-        for cc in range(2):
-            greet(zi * 2 + cc, tensor_of(xi, (yi + d) % ny))
-    for d in range(1, nx):
-        for cc in range(2):
-            greet(zi * 2 + cc, tensor_of((xi + d) % nx, yi))
-    expected = 2 * (nz - 1) + 1 + 2 * (ny - 1) + 2 * (nx - 1)
+    for xx, yy, cc in grid_peers():
+        greet(zi * 2 + cc, tensor_of(xx, yy))
+    expected = 2 * (nz - 1) + 1 + 2 * (nx * ny - 1)
 
     b_lo = pl.multiple_of(xi * STATE, STATE)
     c_lo = pl.multiple_of((groups + xi) * STATE, STATE)
@@ -267,19 +273,23 @@
         ref = buf.at[at, pl.ds(lo, size), :]
         return remote(ref, ref, w_send.at[index], w_recv.at[index], me_r, tt)
 
-    whole = 2 * fill
     load_wa.wait()
     load_wb.wait()
-    wa_up = weight_copy(w_a, yi, 0, whole, 0, tensor_of(xi, up_y))
-    wb_up = weight_copy(w_b, xi, 0, whole, 2, tensor_of(up_x, yi))
-    wa_up.start()
-    wb_up.start()
-    if ny > 2:
-        wa_dn = weight_copy(w_a, yi, 0, whole, 1, tensor_of(xi, dn_y))
-        wa_dn.start()
-    if nx > 2:
-        wb_dn = weight_copy(w_b, xi, 0, whole, 3, tensor_of(dn_x, yi))
-        wb_dn.start()
+    started = []
+
+    def weight_start(copy):
+        copy.start()
+        started.append(copy)
+
+    lows = (0, fill)
+    for turn in range(2):
+        lo, hi = lows[turn], lows[1 - turn]
+        weight_start(weight_copy(w_a, yi, lo, fill, turn, tensor_of(xi, up_y)))
+        weight_start(weight_copy(w_b, xi, lo, fill, 4 + turn, tensor_of(up_x, yi)))
+        if ny > 2:
+            weight_start(weight_copy(w_a, yi, hi, fill, 2 + turn, tensor_of(xi, dn_y)))
+        if nx > 2:
+            weight_start(weight_copy(w_b, xi, hi, fill, 6 + turn, tensor_of(dn_x, yi)))
 
     load_dt.wait()
     head_row = iota((heads, 1), 0)
@@ -353,39 +363,52 @@
         both = recv1[block // 2].astype(F32)
         return jnp.where(block % 2 == 1, both[piece:, :], both[:piece, :])
 
-    def choose(rr, carry):
+    def choose(rr):
         first = pick(prefix_s[2 * rr])
         second = pick(prefix_s[2 * rr + 1])
         send2[rr] = jnp.concatenate([first, second], axis=0).astype(BF16)
-        return carry
-
-    lax.fori_loop(0, nr, choose, 0)
-
-    @pl.when(me_r < tail_n)
-    def _():
-        def choose_tail(rr, carry):
+
+        @pl.when(me_r < tail_n)
+        def _():
             for s in range(2):
                 block = prefix_s[2 * rr + s]
                 both = trecv1[block // 2]
                 tsend2[rr, s * tail_p : (s + 1) * tail_p, :] = jnp.where(
                     block % 2 == 1, both[tail_p:, :], both[:tail_p, :]
                 )
-            return carry
-
-        lax.fori_loop(0, nr, choose_tail, 0)
+
+    def second_copy(rr):
+        return remote(send2.at[rr], recv2.at[me_r], s2_send.at[rr], s2_recv.at[me_r], rr, me_t)
+
+    def second_tail(rr):
+        return remote(tsend2.at[rr], trecv2.at[me_r], t2_send.at[rr], t2_recv.at[me_r], rr, me_t)
 
     def start_second(rr):
-        remote(
-            send2.at[rr], recv2.at[me_r], s2_send.at[rr], s2_recv.at[me_r], rr, me_t
-        ).start()
+        second_copy(rr).start()
 
         @pl.when(me_r < tail_n)
         def _():
-            remote(
-                tsend2.at[rr], trecv2.at[me_r], t2_send.at[rr], t2_recv.at[me_r], rr, me_t
-            ).start()
-
-    each_replica(start_second)
+            second_tail(rr).start()
+
+    def second_step(m, carry):
+        base = far_pair(m)
+        choose(base)
+        choose(base + 1)
+
+        @pl.when(m > 0)
+        def _():
+            before = far_pair(m - 1)
+            start_second(before)
+            start_second(before + 1)
+
+        return carry
+
+    lax.fori_loop(0, nz - 1, second_step, 0)
+    choose(zi * 2)
+    choose(zi * 2 + 1)
+    start_second(far_pair(nz - 2))
+    start_second(far_pair(nz - 2) + 1)
+    start_second(zi * 2 + 1 - ci)
     own2 = pltpu.make_async_copy(send2.at[me_r], recv2.at[me_r], own_sem.at[2])
     own2.start()
 
@@ -398,19 +421,16 @@
     def weight_wait(buf, at, lo, size, index):
         weight_copy(buf, at, lo, size, index, me_t).wait_recv()
 
-    weight_wait(w_a, dn_y, 0, whole, 0)
-    weight_wait(w_b, dn_x, 0, whole, 2)
-    forwards = []
+    weight_wait(w_a, dn_y, 0, fill, 0)
     if ny > 2:
-        weight_wait(w_a, up_y, 0, whole, 1)
-        forwards.append(weight_copy(w_a, dn_y, 0, fill, 4, tensor_of(xi, up_y)))
-        forwards.append(weight_copy(w_a, up_y, fill, fill, 5, tensor_of(xi, dn_y)))
+        weight_start(weight_copy(w_a, dn_y, 0, fill, 8, tensor_of(xi, up_y)))
+        weight_wait(w_a, up_y, fill, fill, 2)
+        weight_start(weight_copy(w_a, up_y, fill, fill, 9, tensor_of(xi, dn_y)))
+    weight_wait(w_b, dn_x, 0, fill, 4)
     if nx > 2:
-        weight_wait(w_b, up_x, 0, whole, 3)
-        forwards.append(weight_copy(w_b, dn_x, 0, fill, 6, tensor_of(up_x, yi)))
-        forwards.append(weight_copy(w_b, up_x, fill, fill, 7, tensor_of(dn_x, yi)))
-    for copy in forwards:
-        copy.start()
+        weight_start(weight_copy(w_b, dn_x, 0, fill, 10, tensor_of(up_x, yi)))
+        weight_wait(w_b, up_x, fill, fill, 6)
+        weight_start(weight_copy(w_b, up_x, fill, fill, 11, tensor_of(dn_x, yi)))
 
     def wait_second(rr):
         remote(send2.at[rr], recv2.at[rr], s2_send.at[rr], s2_recv.at[rr], rr, me_t).wait_recv()
@@ -466,22 +486,23 @@
             )
             y = y + jnp.dot(mixing.astype(BF16), held.astype(BF16), preferred_element_type=F32)
         v = y * gate[q]
-        ss_send[:, q * slot : (q + 1) * slot] = dot_nt(jnp.ones((8, width), F32), v * v, HIGHEST)
+        ss_send[:, q * slot : (q + 1) * slot] = dot_nt(
+            jnp.ones((8, width), F32), v * v, HIGHEST
+        )[0:1]
         live = iota((slot, width), 0) < lengths_s[q]
         v = jnp.where(live, v * gain_v[...], 0.0)
-        v_f[q] = v
         owners = slot // rows_owner // ny
         v_a[q * owners : (q + 1) * owners] = v.astype(BF16).reshape(owners, ny, rows_owner, width)
         saved.append((start_at, xc, b_low))
 
-    def ss_copy(yy, cc):
+    def ss_copy(xx, yy, cc):
         return remote(
             ss_send,
-            ss_recv.at[ci, yi],
-            ss_ssem.at[cc, yy],
-            ss_rsem.at[ci, yi],
-            zi * 2 + cc,
-            tensor_of(xi, yy),
+            ss_recv.at[ci * nx + xi, yi],
+            ss_ssem.at[cc * nx + xx, yy],
+            ss_rsem.at[ci * nx + xi, yi],
+            zi * 2 + cc,
+            tensor_of(xx, yy),
         )
 
     def va_copy(yy, cc):
@@ -494,65 +515,46 @@
             tensor_of(xi, yy),
         )
 
-    for yy, cc in y_peers():
-        ss_copy(yy, cc).start()
-    for yy, cc in y_peers():
-        va_copy(yy, cc).start()
-    ss_recv[ci, yi] = ss_send[...]
+    def vb_copy(xx, cc):
+        return remote(
+            v_a.at[xx],
+            r_b.at[ci, xi],
+            vb_send.at[cc, xx],
+            vb_recv.at[ci, xi],
+            zi * 2 + cc,
+            tensor_of(xx, yi),
+        )
+
+    ss_peers = grid_peers() + [(xi, yi, 1 - ci)]
+    for xx, yy, cc in ss_peers:
+        ss_copy(xx, yy, cc).start()
+    for d in (2, 1, 3, 0):
+        for dc in range(2):
+            if (d or dc) and d < ny:
+                va_copy((yi + d) % ny, (ci + dc) % 2).start()
+            if (d or dc) and d < nx:
+                vb_copy((xi + d) % nx, (ci + dc) % 2).start()
+    ss_recv[ci * nx + xi, yi] = ss_send[...]
     own_a = pltpu.make_async_copy(v_a.at[:, yi], r_a.at[ci, yi], own_sem.at[4])
     own_a.start()
+    own_b = pltpu.make_async_copy(v_a.at[xi], r_b.at[ci, xi], own_sem.at[5])
+    own_b.start()
 
     for q in range(2):
         start_at, xc, b_low = saved[q]
         weighed = (xc * weighin[q]).astype(BF16)
         final_o[q] = ending[q] * start_at + dot_tn(weighed, b_low)
 
-    def ss_wait(yy, cc):
-        remote(
-            ss_send,
-            ss_recv.at[cc, yy],
-            ss_ssem.at[cc, yy],
-            ss_rsem.at[cc, yy],
-            zi * 2 + cc,
-            tensor_of(xi, yy),
-        ).wait_recv()
-
-    for yy, cc in y_peers():
-        ss_wait(yy, cc)
-    scale_t = []
-    for cc in range(2):
-        total = ss_recv[cc, 0]
-        for yy in range(1, ny):
-            total = total + ss_recv[cc, yy]
-        scale_t.append(lax.rsqrt(total / (ny * width) + EPSILON))
-    mine = jnp.where(ci == 0, scale_t[0], scale_t[1])
-    eye_t = (iota((tokens, tokens), 0) == iota((tokens, tokens), 1)).astype(F32)
-    column = dot_nt(eye_t, mine, HIGHEST)
-    for q in range(2):
-        scaled = v_f[q] * column[q * slot : (q + 1) * slot, 0:1]
-        v_b[q * owners : (q + 1) * owners] = scaled.astype(BF16).reshape(
-            owners, ny, rows_owner, width
-        )
-
-    def vb_copy(xx, cc):
-        return remote(
-            v_b.at[xx],
-            r_b.at[ci, xi],
-            vb_send.at[cc, xx],
-            vb_recv.at[ci, xi],
-            zi * 2 + cc,
-            tensor_of(xx, yi),
-        )
-
-    for xx, cc in x_peers():
-        vb_copy(xx, cc).start()
-    own_b = pltpu.make_async_copy(v_b.at[xi], r_b.at[ci, xi], own_sem.at[5])
-    own_b.start()
-
+    if ny > 2:
+        weight_wait(w_a, up_y, 0, fill, 3)
+    weight_wait(w_a, dn_y, fill, fill, 1)
+    if nx > 2:
+        weight_wait(w_b, up_x, 0, fill, 7)
+    weight_wait(w_b, dn_x, fill, fill, 5)
     if ny > 2:
         opp_y = (yi + 2) % ny
-        weight_wait(w_a, opp_y, 0, fill, 4)
-        weight_wait(w_a, opp_y, fill, fill, 5)
+        weight_wait(w_a, opp_y, 0, fill, 8)
+        weight_wait(w_a, opp_y, fill, fill, 9)
     for yy, cc in y_peers():
         remote(
             v_a.at[:, yi],
@@ -568,13 +570,31 @@
     for yy in range(ny):
         lhs = r_a[:, yy].reshape(rows_a, width)
         acc = acc + jnp.dot(lhs, w_a[yy], preferred_element_type=F32)
+    for xx, yy, cc in ss_peers:
+        remote(
+            ss_send,
+            ss_recv.at[cc * nx + xx, yy],
+            ss_ssem.at[cc * nx + xx, yy],
+            ss_rsem.at[cc * nx + xx, yy],
+            zi * 2 + cc,
+            tensor_of(xx, yy),
+        ).wait_recv()
+
+    def scale_row(k):
+        total = ss_recv[k, 0]
+        for yy in range(1, ny):
+            total = total + ss_recv[k, yy]
+        return lax.rsqrt(total / (ny * width) + EPSILON)
+
+    scale_all = jnp.concatenate([scale_row(k) for k in range(2 * nx)], axis=0)
+    scale_mine = jnp.concatenate([scale_row(xi), scale_row(nx + xi)], axis=0)
     per = nx * rows_owner
     where_row = iota((per, tokens), 0)
     wanted = (where_row // rows_owner * ny + yi) * rows_owner + where_row % rows_owner
     pick_rows = (iota((per, tokens), 1) == wanted).astype(F32)
+    col_a = dot_nt(pick_rows, scale_mine, HIGHEST)
     for cc in range(2):
-        col = dot_nt(pick_rows, scale_t[cc], HIGHEST)[:, 0:1]
-        part = acc[cc * per : (cc + 1) * per, :] * col
+        part = acc[cc * per : (cc + 1) * per, :] * col_a[:, cc : cc + 1]
         o_a[cc] = part.astype(BF16).reshape(nx, rows_owner, quarter)
 
     for xx, cc in x_peers():
@@ -591,11 +611,11 @@
 
     if nx > 2:
         opp_x = (xi + 2) % nx
-        weight_wait(w_b, opp_x, 0, fill, 6)
-        weight_wait(w_b, opp_x, fill, fill, 7)
+        weight_wait(w_b, opp_x, 0, fill, 10)
+        weight_wait(w_b, opp_x, fill, fill, 11)
     for xx, cc in x_peers():
         remote(
-            v_b.at[xi],
+            v_a.at[xi],
             r_b.at[cc, xx],
             vb_send.at[cc, xx],
             vb_recv.at[cc, xx],
@@ -605,9 +625,13 @@
     own_b.wait()
     rows_b = 2 * ny * rows_owner
     acc = jnp.zeros((rows_b, quarter), F32)
+    per = ny * rows_owner
+    pick_rows = (iota((per, tokens), 1) == iota((per, tokens), 0) + xi * per).astype(F32)
+    col_b = dot_nt(pick_rows, scale_all, HIGHEST)
     for xx in range(nx):
         lhs = r_b[:, xx].reshape(rows_b, width)
-        acc = acc + jnp.dot(lhs, w_b[xx], preferred_element_type=F32)
+        col = jnp.concatenate([col_b[:, xx : xx + 1], col_b[:, nx + xx : nx + xx + 1]], axis=0)
+        acc = acc + jnp.dot(lhs, w_b[xx], preferred_element_type=F32) * col
     o_b[...] = acc.astype(BF16).reshape(2, ny, rows_owner, quarter)
     for yy, cc in y_peers():
         remote(
@@ -655,9 +679,7 @@
 
     def sent(rr):
         first_copy(rr).wait_send()
-        remote(
-            send2.at[rr], recv2.at[me_r], s2_send.at[rr], s2_recv.at[me_r], rr, me_t
-        ).wait_send()
+        second_copy(rr).wait_send()
 
         @pl.when(rr < tail_n)
         def _():
@@ -665,21 +687,14 @@
 
         @pl.when(me_r < tail_n)
         def _():
-            remote(
-                tsend2.at[rr], trecv2.at[me_r], t2_send.at[rr], t2_recv.at[me_r], rr, me_t
-            ).wait_send()
+            second_tail(rr).wait_send()
 
     each_replica(sent)
-    wa_up.wait_send()
-    wb_up.wait_send()
-    if ny > 2:
-        wa_dn.wait_send()
-    if nx > 2:
-        wb_dn.wait_send()
-    for copy in forwards:
+    for copy in started:
         copy.wait_send()
+    for xx, yy, cc in ss_peers:
+        ss_copy(xx, yy, cc).wait_send()
     for yy, cc in y_peers():
-        ss_copy(yy, cc).wait_send()
         va_copy(yy, cc).wait_send()
         remote(
             o_b.at[cc, yy],
@@ -772,13 +787,11 @@
         vmem((2, slot, width), F32),
         vmem((2, slot, width), F32),
         vmem((2, width, STATE), F32),
-        vmem((2, slot, width), F32),
-        vmem((nx, ny, rows_owner, width), BF16),
         vmem((nx, ny, rows_owner, width), BF16),
         vmem((2, ny, nx, rows_owner, width), BF16),
         vmem((2, nx, ny, rows_owner, width), BF16),
-        vmem((8, tokens), F32),
-        vmem((2, ny, 8, tokens), F32),
+        vmem((1, tokens), F32),
+        vmem((2 * nx, ny, 1, tokens), F32),
         vmem((2, nx, rows_owner, quarter), BF16),
         vmem((2, ny, rows_owner, quarter), BF16),
         vmem((nx, 2, rows_owner, quarter), BF16),
@@ -793,14 +806,14 @@
         dma((nr,)),
         dma((nr,)),
         dma((nr,)),
-        dma((8,)),
-        dma((8,)),
+        dma((12,)),
+        dma((12,)),
         dma((2, ny)),
         dma((2, ny)),
         dma((2, nx)),
         dma((2, nx)),
-        dma((2, ny)),
-        dma((2, ny)),
+        dma((2 * nx, ny)),
+        dma((2 * nx, ny)),
         dma((nx, 2)),
         dma((nx, 2)),
         dma((ny, 2)),

time: 60.1 us -> 57.1 us (0.950)
  Pallas kernels: 59.3 us -> 56.4 us
    pallas_call x1, Pallas kernels: 58.6 us -> 55.6 us  [local(): pl.pallas_call(functools.partial(layer_kernel, sizes), out_shape=(vmem((r...]
where the time goes in v3:
time: 57.1 us; the launch traced here: 57 us
  Pallas kernels  56.4 us (99%)
  between operations  0.64 us (1%)
    pallas_call x1, Pallas kernels, local(): pl.pallas_call(functools.partial(layer_kernel, sizes), out_shape=(vmem((r...  55.6 us

profile of v3, /device:TPU:1, one launch (start us, length us, event | category | flops | bytes accessed | tf_op | source)
XLA Modules:
  0.0 57.0 jit_solution(2054984649444459955)
XLA Ops:
  0.6 55.6 %prefill_layer.1 = (bf16[16,4096]{1,0:T(8,128)(2,1)S(1)}, f32[2,256,128]{2,1,0:T(8,128)S(1)}) custom-call(s32[64]{0:T(128)} %prefix_s.1, s32[2]{0:T(128)} %lengths_s.1, f32[8]{0:T(128)} %bias_s.1, f32[8]{0:T(128)} %rates_s.1, f32[8]{0:T(128)} %skip_s.1, bf16[256,256]{1,0:T(8,128)(2,1)} %x_h.1, bf16[256,256]{1,0:T(8,128)(2,1)} %z_h.1, ...), custom_call_target="tpu_custom_call" | custom-call | tf_op jit(solution)/shard_map/prefill_layer/pallas_call | solution.py:822
  56.2 0.8 %store_results.1 = (bf16[16,4096]{1,0:T(8,128)(2,1)}, f32[2,256,128]{2,1,0:T(8,128)}) custom-call(bf16[16,4096]{1,0:T(8,128)(2,1)S(1)} %get-tuple-element.6.mixed_v, f32[2,256,128]{2,1,0:T(8,128)S(1)} %get-tuple-element.7.final_v), custom_call_target="tpu_custom_call" | custom-call | tf_op jit(solution)/shard_map/store_results/pallas_call | solution.py:850

commit v4 on v3

--- a/solution.py
+++ b/solution.py
@@ -38,11 +38,11 @@
 
 def layer_kernel(
     sizes,
-    prefix_s,
-    lengths_s,
-    bias_s,
-    rates_s,
-    skip_s,
+    prefix_h,
+    lengths_h,
+    bias_h,
+    rates_h,
+    skip_h,
     x_h,
     z_h,
     bc_h,
@@ -56,6 +56,11 @@
     tailbc_h,
     mixed_o,
     final_o,
+    prefix_s,
+    lengths_s,
+    bias_s,
+    rates_s,
+    skip_s,
     x_v,
     z_v,
     bc_v,
@@ -176,6 +181,12 @@
     def tensor_of(xx, yy):
         return xx * ny + yy
 
+    def tail_slot(rr):
+        return (rr * tail_n + nr - 1) // nr
+
+    def has_tail(rr):
+        return tail_slot(rr) * nr // tail_n == rr
+
     def remote(src, dst, ssem, rsem, rr, tt):
         return pltpu.make_async_remote_copy(
             src_ref=src,
@@ -211,6 +222,13 @@
 
     load_states = load(states_h, st_v)
     load_tx = load(tailx_h, tailx_v)
+    scalars = [
+        load(prefix_h, prefix_s),
+        load(lengths_h, lengths_s),
+        load(bias_h, bias_s),
+        load(rates_h, rates_s),
+        load(skip_h, skip_s),
+    ]
     load_tb = load(tailbc_h.at[:, :, pl.ds(b_lo, STATE)], tailbc_v.at[:, :, lane_b])
     load_tc = load(tailbc_h.at[:, :, pl.ds(c_lo, STATE)], tailbc_v.at[:, :, lane_c])
     load_dt = load(dt_h, dt_v)
@@ -240,18 +258,20 @@
             at = b * tail_p + row % tail_p
             tsend1[row // tail_p, at : at + 1, :] = src[t, b : b + 1, lanes]
 
+    for copy in scalars:
+        copy.wait()
     pl.semaphore_wait(barrier, expected)
 
     def first_copy(rr):
         return remote(send1.at[rr], recv1.at[me_r], s1_send.at[rr], s1_recv.at[me_r], rr, me_t)
 
     def first_tail(rr):
-        return remote(tsend1.at[rr], trecv1.at[me_r], t1_send.at[rr], t1_recv.at[me_r], rr, me_t)
+        return remote(tsend1.at[tail_slot(rr)], trecv1.at[me_r], t1_send.at[rr], t1_recv.at[me_r], rr, me_t)
 
     def start_first(rr):
         first_copy(rr).start()
 
-        @pl.when(rr < tail_n)
+        @pl.when(has_tail(rr))
         def _():
             first_tail(rr).start()
 
@@ -259,9 +279,11 @@
     own1 = pltpu.make_async_copy(send1.at[me_r], recv1.at[me_r], own_sem.at[0])
     own1.start()
 
-    @pl.when(me_r < tail_n)
+    @pl.when(has_tail(me_r))
     def _():
-        copy = pltpu.make_async_copy(tsend1.at[me_r], trecv1.at[me_r], own_sem.at[1])
+        copy = pltpu.make_async_copy(
+            tsend1.at[tail_slot(me_r)], trecv1.at[me_r], own_sem.at[1]
+        )
         copy.start()
         copy.wait()
 
@@ -290,6 +312,122 @@
             weight_start(weight_copy(w_a, yi, hi, fill, 2 + turn, tensor_of(xi, dn_y)))
         if nx > 2:
             weight_start(weight_copy(w_b, xi, hi, fill, 6 + turn, tensor_of(dn_x, yi)))
+
+    def raw_conv(seq, taps):
+        total = seq * taps[3:4, :]
+        at = iota(seq.shape, 0)
+        for n in range(1, 4):
+            moved = jnp.where(at >= n, pltpu.roll(seq, n, 0), 0.0)
+            total = total + moved * taps[3 - n : 4 - n, :]
+        return total
+
+    load_x.wait()
+    load_cx.wait()
+    load_b.wait()
+    load_c.wait()
+    load_cb.wait()
+    load_cc.wait()
+    load_z.wait()
+    for q in range(2):
+        part = slice(q * slot, (q + 1) * slot)
+        xraw[q] = raw_conv(x_v[part, :].astype(F32), convx_v[...])
+        bcraw[q] = raw_conv(bc_v[part, :].astype(F32), convbc_v[...])
+        gate[q] = silu(z_v[part, :].astype(F32))
+    load_g.wait()
+
+    def wait_first(rr):
+        remote(send1.at[rr], recv1.at[rr], s1_send.at[rr], s1_recv.at[rr], rr, me_t).wait_recv()
+
+        @pl.when(has_tail(me_r))
+        def _():
+            remote(
+                tsend1.at[0], trecv1.at[rr], t1_send.at[0], t1_recv.at[rr], rr, me_t
+            ).wait_recv()
+
+    own1.wait()
+    each_replica(wait_first)
+
+    def pick(block):
+        both = recv1[block // 2].astype(F32)
+        return jnp.where(block % 2 == 1, both[piece:, :], both[:piece, :])
+
+    def choose(rr):
+        first = pick(prefix_s[2 * rr])
+        second = pick(prefix_s[2 * rr + 1])
+        send2[rr] = jnp.concatenate([first, second], axis=0).astype(BF16)
+
+        @pl.when(has_tail(me_r))
+        def _():
+            for s in range(2):
+                block = prefix_s[2 * rr + s]
+                both = trecv1[block // 2]
+                tsend2[rr, s * tail_p : (s + 1) * tail_p, :] = jnp.where(
+                    block % 2 == 1, both[tail_p:, :], both[:tail_p, :]
+                )
+
+    def second_copy(rr):
+        return remote(send2.at[rr], recv2.at[me_r], s2_send.at[rr], s2_recv.at[me_r], rr, me_t)
+
+    def second_tail(rr):
+        return remote(
+            tsend2.at[rr],
+            trecv2.at[tail_slot(me_r)],
+            t2_send.at[rr],
+            t2_recv.at[tail_slot(me_r)],
+            rr,
+            me_t,
+        )
+
+    def start_second(rr):
+        second_copy(rr).start()
+
+        @pl.when(has_tail(me_r))
+        def _():
+            second_tail(rr).start()
+
+    def second_step(m, carry):
+        base = far_pair(m)
+        choose(base)
+        choose(base + 1)
+
+        @pl.when(m > 0)
+        def _():
+            before = far_pair(m - 1)
+            start_second(before)
+            start_second(before + 1)
+
+        return carry
+
+    lax.fori_loop(0, nz - 1, second_step, 0)
+    choose(zi * 2)
+    choose(zi * 2 + 1)
+    start_second(far_pair(nz - 2))
+    start_second(far_pair(nz - 2) + 1)
+    start_second(zi * 2 + 1 - ci)
+    own2 = pltpu.make_async_copy(send2.at[me_r], recv2.at[me_r], own_sem.at[2])
+    own2.start()
+
+    @pl.when(has_tail(me_r))
+    def _():
+        copy = pltpu.make_async_copy(
+            tsend2.at[me_r], trecv2.at[tail_slot(me_r)], own_sem.at[3]
+        )
+        copy.start()
+        copy.wait()
+
+    def weight_wait(buf, at, lo, size, index):
+        weight_copy(buf, at, lo, size, index, me_t).wait_recv()
+
+    weight_wait(w_a, dn_y, 0, fill, 0)
+    if ny > 2:
+        weight_start(weight_copy(w_a, dn_y, 0, fill, 8, tensor_of(xi, up_y)))
+        weight_wait(w_a, up_y, fill, fill, 2)
+        weight_start(weight_copy(w_a, up_y, fill, fill, 9, tensor_of(xi, dn_y)))
+    weight_wait(w_b, dn_x, 0, fill, 4)
+    if nx > 2:
+        weight_start(weight_copy(w_b, dn_x, 0, fill, 10, tensor_of(up_x, yi)))
+        weight_wait(w_b, up_x, fill, fill, 6)
+        weight_start(weight_copy(w_b, up_x, fill, fill, 11, tensor_of(dn_x, yi)))
 
     load_dt.wait()
     head_row = iota((heads, 1), 0)
@@ -325,120 +463,18 @@
         ending[q] = dot_tn(spread, jnp.broadcast_to(jnp.exp(last), (heads, STATE)), HIGHEST)
     skip_wide = jnp.dot(skip_row, spread, precision=HIGHEST, preferred_element_type=F32)
 
-    def raw_conv(seq, taps):
-        total = seq * taps[3:4, :]
-        at = iota(seq.shape, 0)
-        for n in range(1, 4):
-            moved = jnp.where(at >= n, pltpu.roll(seq, n, 0), 0.0)
-            total = total + moved * taps[3 - n : 4 - n, :]
-        return total
-
-    load_x.wait()
-    load_cx.wait()
-    load_b.wait()
-    load_c.wait()
-    load_cb.wait()
-    load_cc.wait()
-    load_z.wait()
-    for q in range(2):
-        part = slice(q * slot, (q + 1) * slot)
-        xraw[q] = raw_conv(x_v[part, :].astype(F32), convx_v[...])
-        bcraw[q] = raw_conv(bc_v[part, :].astype(F32), convbc_v[...])
-        gate[q] = silu(z_v[part, :].astype(F32))
-    load_g.wait()
-
-    def wait_first(rr):
-        remote(send1.at[rr], recv1.at[rr], s1_send.at[rr], s1_recv.at[rr], rr, me_t).wait_recv()
-
-        @pl.when(me_r < tail_n)
+    def wait_second(rr):
+        remote(send2.at[rr], recv2.at[rr], s2_send.at[rr], s2_recv.at[rr], rr, me_t).wait_recv()
+
+        @pl.when(has_tail(rr))
         def _():
             remote(
-                tsend1.at[0], trecv1.at[rr], t1_send.at[0], t1_recv.at[rr], rr, me_t
-            ).wait_recv()
-
-    own1.wait()
-    each_replica(wait_first)
-
-    def pick(block):
-        both = recv1[block // 2].astype(F32)
-        return jnp.where(block % 2 == 1, both[piece:, :], both[:piece, :])
-
-    def choose(rr):
-        first = pick(prefix_s[2 * rr])
-        second = pick(prefix_s[2 * rr + 1])
-        send2[rr] = jnp.concatenate([first, second], axis=0).astype(BF16)
-
-        @pl.when(me_r < tail_n)
-        def _():
-            for s in range(2):
-                block = prefix_s[2 * rr + s]
-                both = trecv1[block // 2]
-                tsend2[rr, s * tail_p : (s + 1) * tail_p, :] = jnp.where(
-                    block % 2 == 1, both[tail_p:, :], both[:tail_p, :]
-                )
-
-    def second_copy(rr):
-        return remote(send2.at[rr], recv2.at[me_r], s2_send.at[rr], s2_recv.at[me_r], rr, me_t)
-
-    def second_tail(rr):
-        return remote(tsend2.at[rr], trecv2.at[me_r], t2_send.at[rr], t2_recv.at[me_r], rr, me_t)
-
-    def start_second(rr):
-        second_copy(rr).start()
-
-        @pl.when(me_r < tail_n)
-        def _():
-            second_tail(rr).start()
-
-    def second_step(m, carry):
-        base = far_pair(m)
-        choose(base)
-        choose(base + 1)
-
-        @pl.when(m > 0)
-        def _():
-            before = far_pair(m - 1)
-            start_second(before)
-            start_second(before + 1)
-
-        return carry
-
-    lax.fori_loop(0, nz - 1, second_step, 0)
-    choose(zi * 2)
-    choose(zi * 2 + 1)
-    start_second(far_pair(nz - 2))
-    start_second(far_pair(nz - 2) + 1)
-    start_second(zi * 2 + 1 - ci)
-    own2 = pltpu.make_async_copy(send2.at[me_r], recv2.at[me_r], own_sem.at[2])
-    own2.start()
-
-    @pl.when(me_r < tail_n)
-    def _():
-        copy = pltpu.make_async_copy(tsend2.at[me_r], trecv2.at[me_r], own_sem.at[3])
-        copy.start()
-        copy.wait()
-
-    def weight_wait(buf, at, lo, size, index):
-        weight_copy(buf, at, lo, size, index, me_t).wait_recv()
-
-    weight_wait(w_a, dn_y, 0, fill, 0)
-    if ny > 2:
-        weight_start(weight_copy(w_a, dn_y, 0, fill, 8, tensor_of(xi, up_y)))
-        weight_wait(w_a, up_y, fill, fill, 2)
-        weight_start(weight_copy(w_a, up_y, fill, fill, 9, tensor_of(xi, dn_y)))
-    weight_wait(w_b, dn_x, 0, fill, 4)
-    if nx > 2:
-        weight_start(weight_copy(w_b, dn_x, 0, fill, 10, tensor_of(up_x, yi)))
-        weight_wait(w_b, up_x, fill, fill, 6)
-        weight_start(weight_copy(w_b, up_x, fill, fill, 11, tensor_of(dn_x, yi)))
-
-    def wait_second(rr):
-        remote(send2.at[rr], recv2.at[rr], s2_send.at[rr], s2_recv.at[rr], rr, me_t).wait_recv()
-
-        @pl.when(rr < tail_n)
-        def _():
-            remote(
-                tsend2.at[0], trecv2.at[rr], t2_send.at[0], t2_recv.at[rr], rr, me_t
+                tsend2.at[0],
+                trecv2.at[tail_slot(rr)],
+                t2_send.at[0],
+                t2_recv.at[tail_slot(rr)],
+                rr,
+                me_t,
             ).wait_recv()
 
     own2.wait()
@@ -545,31 +581,55 @@
         weighed = (xc * weighin[q]).astype(BF16)
         final_o[q] = ending[q] * start_at + dot_tn(weighed, b_low)
 
+    def wait_va(yy, cores):
+        for cc in cores:
+            remote(
+                v_a.at[:, yi],
+                r_a.at[cc, yy],
+                va_send.at[cc, yy],
+                va_recv.at[cc, yy],
+                zi * 2 + cc,
+                tensor_of(xi, yy),
+            ).wait_recv()
+
+    def wait_vb(xx, cores):
+        for cc in cores:
+            remote(
+                v_a.at[xi],
+                r_b.at[cc, xx],
+                vb_send.at[cc, xx],
+                vb_recv.at[cc, xx],
+                zi * 2 + cc,
+                tensor_of(xx, yi),
+            ).wait_recv()
+
+    per_a = nx * rows_owner
+    per_b = ny * rows_owner
+
+    half = quarter // 2
+    x_order = x_peers()[::-1]
+    y_order = y_peers()[::-1]
+    if nx > 2:
+        x_order = [((xi + d) % nx, (ci + e) % 2) for d in (2, 1, 3) for e in range(2)]
+        x_order.append((xi, 1 - ci))
     if ny > 2:
-        weight_wait(w_a, up_y, 0, fill, 3)
-    weight_wait(w_a, dn_y, fill, fill, 1)
-    if nx > 2:
-        weight_wait(w_b, up_x, 0, fill, 7)
-    weight_wait(w_b, dn_x, fill, fill, 5)
-    if ny > 2:
-        opp_y = (yi + 2) % ny
-        weight_wait(w_a, opp_y, 0, fill, 8)
-        weight_wait(w_a, opp_y, fill, fill, 9)
-    for yy, cc in y_peers():
-        remote(
-            v_a.at[:, yi],
-            r_a.at[cc, yy],
-            va_send.at[cc, yy],
-            va_recv.at[cc, yy],
-            zi * 2 + cc,
-            tensor_of(xi, yy),
-        ).wait_recv()
-    own_a.wait()
-    rows_a = 2 * nx * rows_owner
-    acc = jnp.zeros((rows_a, quarter), F32)
-    for yy in range(ny):
-        lhs = r_a[:, yy].reshape(rows_a, width)
-        acc = acc + jnp.dot(lhs, w_a[yy], preferred_element_type=F32)
+        y_order = [((yi + d) % ny, (ci + e) % 2) for d in (2, 1, 3) for e in range(2)]
+        y_order.append((yi, 1 - ci))
+
+    def block_a(yy, cols):
+        lhs = jnp.concatenate(
+            [r_a[0, yy].reshape(per_a, width), r_a[1, yy].reshape(per_a, width)], axis=0
+        )
+        return jnp.dot(lhs, w_a[yy, :, cols], preferred_element_type=F32)
+
+    def block_b(at, cols):
+        xx = at
+        lhs = jnp.concatenate(
+            [r_b[0, xx].reshape(per_b, width), r_b[1, xx].reshape(per_b, width)], axis=0
+        )
+        col = jnp.concatenate([col_b[:, at : at + 1], col_b[:, nx + at : nx + at + 1]], axis=0)
+        return jnp.dot(lhs, w_b[xx, :, cols], preferred_element_type=F32) * col
+
     for xx, yy, cc in ss_peers:
         remote(
             ss_send,
@@ -584,108 +644,131 @@
         total = ss_recv[k, 0]
         for yy in range(1, ny):
             total = total + ss_recv[k, yy]
-        return lax.rsqrt(total / (ny * width) + EPSILON)
-
-    scale_all = jnp.concatenate([scale_row(k) for k in range(2 * nx)], axis=0)
+        return total
+
+    scale_all = jnp.concatenate(
+        [scale_row(cc * nx + xx) for cc in range(2) for xx in range(nx)], axis=0
+    )
+    scale_all = lax.rsqrt(scale_all / (ny * width) + EPSILON)
+    pick_b = (iota((per_b, tokens), 1) == iota((per_b, tokens), 0) + xi * per_b).astype(F32)
+    col_b = dot_nt(pick_b, scale_all, HIGHEST)
+    where_row = iota((per_a, tokens), 0)
+    wanted = (where_row // rows_owner * ny + yi) * rows_owner + where_row % rows_owner
+    pick_a = (iota((per_a, tokens), 1) == wanted).astype(F32)
     scale_mine = jnp.concatenate([scale_row(xi), scale_row(nx + xi)], axis=0)
-    per = nx * rows_owner
-    where_row = iota((per, tokens), 0)
-    wanted = (where_row // rows_owner * ny + yi) * rows_owner + where_row % rows_owner
-    pick_rows = (iota((per, tokens), 1) == wanted).astype(F32)
-    col_a = dot_nt(pick_rows, scale_mine, HIGHEST)
-    for cc in range(2):
-        part = acc[cc * per : (cc + 1) * per, :] * col_a[:, cc : cc + 1]
-        o_a[cc] = part.astype(BF16).reshape(nx, rows_owner, quarter)
-
-    for xx, cc in x_peers():
-        remote(
-            o_a.at[cc, xx],
-            ro_a.at[xi, ci],
-            oa_send.at[xx, cc],
-            oa_recv.at[xi, ci],
-            zi * 2 + cc,
-            tensor_of(xx, yi),
-        ).start()
-    own_oa = pltpu.make_async_copy(o_a.at[ci, xi], ro_a.at[xi, ci], own_sem.at[6])
-    own_oa.start()
-
+    scale_mine = lax.rsqrt(scale_mine / (ny * width) + EPSILON)
+    col_a = dot_nt(pick_a, scale_mine, HIGHEST)
+
+    weight_wait(w_a, dn_y, fill, fill, 1)
+    if ny > 2:
+        weight_wait(w_a, up_y, 0, fill, 3)
+        opp_y = (yi + 2) % ny
+        weight_wait(w_a, opp_y, 0, fill, 8)
+        weight_wait(w_a, opp_y, fill, fill, 9)
+    for yy, cc in y_peers():
+        wait_va(yy, (cc,))
+    own_a.wait()
+    own_b.wait()
+    wait_vb(xi, (1 - ci,))
+    weight_wait(w_b, dn_x, fill, fill, 5)
     if nx > 2:
+        weight_wait(w_b, up_x, 0, fill, 7)
         opp_x = (xi + 2) % nx
         weight_wait(w_b, opp_x, 0, fill, 10)
         weight_wait(w_b, opp_x, fill, fill, 11)
-    for xx, cc in x_peers():
-        remote(
-            v_a.at[xi],
-            r_b.at[cc, xx],
-            vb_send.at[cc, xx],
-            vb_recv.at[cc, xx],
+    for xx, cc in x_peers()[1:]:
+        wait_vb(xx, (cc,))
+
+    def oa_copy(h, xx, cc):
+        return remote(
+            o_a.at[h, cc, xx],
+            ro_a.at[h, xi, ci],
+            oa_send.at[h, xx, cc],
+            oa_recv.at[h, xi, ci],
             zi * 2 + cc,
             tensor_of(xx, yi),
-        ).wait_recv()
-    own_b.wait()
-    rows_b = 2 * ny * rows_owner
-    acc = jnp.zeros((rows_b, quarter), F32)
-    per = ny * rows_owner
-    pick_rows = (iota((per, tokens), 1) == iota((per, tokens), 0) + xi * per).astype(F32)
-    col_b = dot_nt(pick_rows, scale_all, HIGHEST)
-    for xx in range(nx):
-        lhs = r_b[:, xx].reshape(rows_b, width)
-        col = jnp.concatenate([col_b[:, xx : xx + 1], col_b[:, nx + xx : nx + xx + 1]], axis=0)
-        acc = acc + jnp.dot(lhs, w_b[xx], preferred_element_type=F32) * col
-    o_b[...] = acc.astype(BF16).reshape(2, ny, rows_owner, quarter)
-    for yy, cc in y_peers():
-        remote(
-            o_b.at[cc, yy],
-            ro_b.at[yi, ci],
-            ob_send.at[yy, cc],
-            ob_recv.at[yi, ci],
+        )
+
+    def ob_copy(h, yy, cc):
+        return remote(
+            o_b.at[h, cc, yy],
+            ro_b.at[h, yi, ci],
+            ob_send.at[h, yy, cc],
+            ob_recv.at[h, yi, ci],
             zi * 2 + cc,
             tensor_of(xi, yy),
-        ).start()
-    own_ob = pltpu.make_async_copy(o_b.at[ci, yi], ro_b.at[yi, ci], own_sem.at[7])
-    own_ob.start()
-
-    for xx, cc in x_peers():
-        remote(
-            o_a.at[cc, xx],
-            ro_a.at[xx, cc],
-            oa_send.at[xx, cc],
-            oa_recv.at[xx, cc],
-            zi * 2 + cc,
-            tensor_of(xx, yi),
-        ).wait_recv()
-    own_oa.wait()
-    for cc in range(2):
-        total = ro_a[0, cc].astype(F32)
-        for xx in range(1, nx):
-            total = total + ro_a[xx, cc].astype(F32)
-        mixed_o[:, cc * quarter : (cc + 1) * quarter] = total.astype(BF16)
-    for yy, cc in y_peers():
-        remote(
-            o_b.at[cc, yy],
-            ro_b.at[yy, cc],
-            ob_send.at[yy, cc],
-            ob_recv.at[yy, cc],
-            zi * 2 + cc,
-            tensor_of(xi, yy),
-        ).wait_recv()
-    own_ob.wait()
-    for cc in range(2):
-        total = ro_b[0, cc].astype(F32)
+        )
+
+    for h in range(2):
+        cols = slice(h * half, (h + 1) * half)
+        total = block_a(0, cols)
         for yy in range(1, ny):
-            total = total + ro_b[yy, cc].astype(F32)
-        lo = half_cols + cc * quarter
-        mixed_o[:, lo : lo + quarter] = total.astype(BF16)
+            total = total + block_a(yy, cols)
+        for cc in range(2):
+            part = total[cc * per_a : (cc + 1) * per_a, :] * col_a[:, cc : cc + 1]
+            o_a[h, cc] = part.astype(BF16).reshape(nx, rows_owner, half)
+        for xx, cc in x_order:
+            oa_copy(h, xx, cc).start()
+        total = block_b(0, cols)
+        for at in range(1, nx):
+            total = total + block_b(at, cols)
+        o_b[h] = total.astype(BF16).reshape(2, ny, rows_owner, half)
+        for yy, cc in y_order:
+            ob_copy(h, yy, cc).start()
+    own_out = []
+    for h in range(2):
+        own_out.append(
+            pltpu.make_async_copy(o_a.at[h, ci, xi], ro_a.at[h, xi, ci], own_sem.at[6 + h])
+        )
+        own_out.append(
+            pltpu.make_async_copy(o_b.at[h, ci, yi], ro_b.at[h, yi, ci], own_sem.at[8 + h])
+        )
+    for copy in own_out:
+        copy.start()
+    for copy in own_out:
+        copy.wait()
+
+    for h in range(2):
+        for xx, cc in x_peers():
+            remote(
+                o_a.at[h, cc, xx],
+                ro_a.at[h, xx, cc],
+                oa_send.at[h, xx, cc],
+                oa_recv.at[h, xx, cc],
+                zi * 2 + cc,
+                tensor_of(xx, yi),
+            ).wait_recv()
+        for cc in range(2):
+            total = ro_a[h, 0, cc].astype(F32)
+            for xx in range(1, nx):
+                total = total + ro_a[h, xx, cc].astype(F32)
+            lo = cc * quarter + h * half
+            mixed_o[:, lo : lo + half] = total.astype(BF16)
+        for yy, cc in y_peers():
+            remote(
+                o_b.at[h, cc, yy],
+                ro_b.at[h, yy, cc],
+                ob_send.at[h, yy, cc],
+                ob_recv.at[h, yy, cc],
+                zi * 2 + cc,
+                tensor_of(xi, yy),
+            ).wait_recv()
+        for cc in range(2):
+            total = ro_b[h, 0, cc].astype(F32)
+            for yy in range(1, ny):
+                total = total + ro_b[h, yy, cc].astype(F32)
+            lo = half_cols + cc * quarter + h * half
+            mixed_o[:, lo : lo + half] = total.astype(BF16)
 
     def sent(rr):
         first_copy(rr).wait_send()
         second_copy(rr).wait_send()
 
-        @pl.when(rr < tail_n)
+        @pl.when(has_tail(rr))
         def _():
             first_tail(rr).wait_send()
 
-        @pl.when(me_r < tail_n)
+        @pl.when(has_tail(me_r))
         def _():
             second_tail(rr).wait_send()
 
@@ -696,24 +779,12 @@
         ss_copy(xx, yy, cc).wait_send()
     for yy, cc in y_peers():
         va_copy(yy, cc).wait_send()
-        remote(
-            o_b.at[cc, yy],
-            ro_b.at[yi, ci],
-            ob_send.at[yy, cc],
-            ob_recv.at[yi, ci],
-            zi * 2 + cc,
-            tensor_of(xi, yy),
-        ).wait_send()
+        for h in range(2):
+            ob_copy(h, yy, cc).wait_send()
     for xx, cc in x_peers():
         vb_copy(xx, cc).wait_send()
-        remote(
-            o_a.at[cc, xx],
-            ro_a.at[xi, ci],
-            oa_send.at[xx, cc],
-            oa_recv.at[xi, ci],
-            zi * 2 + cc,
-            tensor_of(xx, yi),
-        ).wait_send()
+        for h in range(2):
+            oa_copy(h, xx, cc).wait_send()
 
 
 def store_kernel(mixed_v, final_v, mixed_o, final_o, sem):
@@ -756,10 +827,15 @@
     tail_p = TAIL_ROWS // tail_n
     vmem = pltpu.VMEM
     dma = pltpu.SemaphoreType.DMA
-    smem_spec = pl.BlockSpec(memory_space=pltpu.SMEM)
+    smem = pltpu.SMEM
     hbm_spec = pl.BlockSpec(memory_space=pl.ANY)
     vmem_spec = pl.BlockSpec(memory_space=pltpu.VMEM)
     scratch = [
+        smem(prefix_block.shape, jnp.int32),
+        smem(lengths.shape, jnp.int32),
+        smem((heads,), F32),
+        smem((heads,), F32),
+        smem((heads,), F32),
         vmem((tokens, width), BF16),
         vmem((tokens, width), BF16),
         vmem((tokens, 2 * STATE), BF16),
@@ -792,12 +868,12 @@
         vmem((2, nx, ny, rows_owner, width), BF16),
         vmem((1, tokens), F32),
         vmem((2 * nx, ny, 1, tokens), F32),
-        vmem((2, nx, rows_owner, quarter), BF16),
-        vmem((2, ny, rows_owner, quarter), BF16),
-        vmem((nx, 2, rows_owner, quarter), BF16),
-        vmem((ny, 2, rows_owner, quarter), BF16),
-        dma((15,)),
-        dma((8,)),
+        vmem((2, 2, nx, rows_owner, quarter // 2), BF16),
+        vmem((2, 2, ny, rows_owner, quarter // 2), BF16),
+        vmem((2, nx, 2, rows_owner, quarter // 2), BF16),
+        vmem((2, ny, 2, rows_owner, quarter // 2), BF16),
+        dma((20,)),
+        dma((10,)),
         dma((nr,)),
         dma((nr,)),
         dma((nr,)),
@@ -814,15 +890,15 @@
         dma((2, nx)),
         dma((2 * nx, ny)),
         dma((2 * nx, ny)),
-        dma((nx, 2)),
-        dma((nx, 2)),
-        dma((ny, 2)),
-        dma((ny, 2)),
+        dma((2, nx, 2)),
+        dma((2, nx, 2)),
+        dma((2, ny, 2)),
+        dma((2, ny, 2)),
     ]
     mixed, final_states = pl.pallas_call(
         functools.partial(layer_kernel, sizes),
         out_shape=(vmem((rows_owner, out_cols), BF16), vmem((2, width, STATE), F32)),
-        in_specs=[smem_spec] * 5 + [hbm_spec] * 11,
+        in_specs=[hbm_spec] * 16,
         out_specs=(vmem_spec, vmem_spec),
         scratch_shapes=scratch,
         compiler_params=pltpu.CompilerParams(

time: 57.1 us -> 57 us (level)
  no operation moved by 1% of the time
where the time goes in v4:
time: 57 us; the launch traced here: 56.8 us
  Pallas kernels  56.2 us (99%)
  between operations  0.64 us (1%)
    pallas_call x1, Pallas kernels, local(): pl.pallas_call(functools.partial(layer_kernel, sizes), out_shape=(vmem((r...  55.4 us

profile of v4, /device:TPU:1, one launch (start us, length us, event | category | flops | bytes accessed | tf_op | source)
XLA Modules:
  0.0 56.8 jit_solution(10620834897893815496)
XLA Ops:
  0.6 55.4 %prefill_layer.1 = (bf16[16,4096]{1,0:T(8,128)(2,1)S(1)}, f32[2,256,128]{2,1,0:T(8,128)S(1)}) custom-call(s32[64]{0:T(128)} %prefix_h.1, s32[2]{0:T(128)} %lengths_h.1, f32[8]{0:T(128)} %bias_h.1, f32[8]{0:T(128)} %rates_h.1, f32[8]{0:T(128)} %skip_h.1, bf16[256,256]{1,0:T(8,128)(2,1)} %x_h.1, bf16[256,256]{1,0:T(8,128)(2,1)} %z_h.1, ...), custom_call_target="tpu_custom_call" | custom-call | tf_op jit(solution)/shard_map/prefill_layer/pallas_call | solution.py:898
  56.1 0.8 %store_results.1 = (bf16[16,4096]{1,0:T(8,128)(2,1)}, f32[2,256,128]{2,1,0:T(8,128)}) custom-call(bf16[16,4096]{1,0:T(8,128)(2,1)S(1)} %get-tuple-element.6.mixed_v, f32[2,256,128]{2,1,0:T(8,128)S(1)} %get-tuple-element.7.final_v), custom_call_target="tpu_custom_call" | custom-call | tf_op jit(solution)/shard_map/store_results/pallas_call | solution.py:926

commit v5 on v4

--- a/solution.py
+++ b/solution.py
@@ -250,13 +250,15 @@
     load_tx.wait()
     load_tb.wait()
     load_tc.wait()
-    for row in range(TAIL_ROWS):
-        t, part = row // 4, row % 4
+    for j in range(tail_n):
+        lines = []
         for b in range(2):
-            src = tailx_v if part < 2 else tailbc_v
-            lanes = slice((part % 2) * STATE, (part % 2 + 1) * STATE)
-            at = b * tail_p + row % tail_p
-            tsend1[row // tail_p, at : at + 1, :] = src[t, b : b + 1, lanes]
+            for row in range(j * tail_p, (j + 1) * tail_p):
+                t, part = row // 4, row % 4
+                src = tailx_v if part < 2 else tailbc_v
+                lanes = slice((part % 2) * STATE, (part % 2 + 1) * STATE)
+                lines.append(src[t, b : b + 1, lanes])
+        tsend1[j] = jnp.concatenate(lines, axis=0).astype(BF16)
 
     for copy in scalars:
         copy.wait()
@@ -358,12 +360,12 @@
 
         @pl.when(has_tail(me_r))
         def _():
+            chosen = []
             for s in range(2):
                 block = prefix_s[2 * rr + s]
-                both = trecv1[block // 2]
-                tsend2[rr, s * tail_p : (s + 1) * tail_p, :] = jnp.where(
-                    block % 2 == 1, both[tail_p:, :], both[:tail_p, :]
-                )
+                both = trecv1[block // 2].astype(F32)
+                chosen.append(jnp.where(block % 2 == 1, both[tail_p:, :], both[:tail_p, :]))
+            tsend2[rr] = jnp.concatenate(chosen, axis=0).astype(BF16)
 
     def second_copy(rr):
         return remote(send2.at[rr], recv2.at[me_r], s2_send.at[rr], s2_recv.at[me_r], rr, me_t)
@@ -492,7 +494,7 @@
             for t in range(3):
                 row = t * 4 + part
                 at = q * tail_p + row % tail_p
-                line = trecv2[row // tail_p, at : at + 1, :]
+                line = trecv2[row // tail_p].astype(F32)[at : at + 1, :]
                 tile = jnp.where(at8 == t, line, tile)
             return tile
 
@@ -727,6 +729,28 @@
         copy.start()
     for copy in own_out:
         copy.wait()
+
+    def sent(rr):
+        first_copy(rr).wait_send()
+        second_copy(rr).wait_send()
+
+        @pl.when(has_tail(rr))
+        def _():
+            first_tail(rr).wait_send()
+
+        @pl.when(has_tail(me_r))
+        def _():
+            second_tail(rr).wait_send()
+
+    each_replica(sent)
+    for copy in started:
+        copy.wait_send()
+    for xx, yy, cc in ss_peers:
+        ss_copy(xx, yy, cc).wait_send()
+    for yy, cc in y_peers():
+        va_copy(yy, cc).wait_send()
+    for xx, cc in x_peers():
+        vb_copy(xx, cc).wait_send()
 
     for h in range(2):
         for xx, cc in x_peers():
@@ -760,30 +784,10 @@
             lo = half_cols + cc * quarter + h * half
             mixed_o[:, lo : lo + half] = total.astype(BF16)
 
-    def sent(rr):
-        first_copy(rr).wait_send()
-        second_copy(rr).wait_send()
-
-        @pl.when(has_tail(rr))
-        def _():
-            first_tail(rr).wait_send()
-
-        @pl.when(has_tail(me_r))
-        def _():
-            second_tail(rr).wait_send()
-
-    each_replica(sent)
-    for copy in started:
-        copy.wait_send()
-    for xx, yy, cc in ss_peers:
-        ss_copy(xx, yy, cc).wait_send()
-    for yy, cc in y_peers():
-        va_copy(yy, cc).wait_send()
-        for h in range(2):
+    for h in range(2):
+        for yy, cc in y_peers():
             ob_copy(h, yy, cc).wait_send()
-    for xx, cc in x_peers():
-        vb_copy(xx, cc).wait_send()
-        for h in range(2):
+        for xx, cc in x_peers():
             oa_copy(h, xx, cc).wait_send()
 
 
@@ -850,10 +854,10 @@
         vmem((nr, 2 * piece, STATE), BF16),
         vmem((nr, 2 * piece, STATE), BF16),
         vmem((nr, 2 * piece, STATE), BF16),
-        vmem((tail_n, 2 * tail_p, STATE), F32),
-        vmem((nr, 2 * tail_p, STATE), F32),
-        vmem((nr, 2 * tail_p, STATE), F32),
-        vmem((tail_n, 2 * tail_p, STATE), F32),
+        vmem((tail_n, 2 * tail_p, STATE), BF16),
+        vmem((nr, 2 * tail_p, STATE), BF16),
+        vmem((nr, 2 * tail_p, STATE), BF16),
+        vmem((tail_n, 2 * tail_p, STATE), BF16),
         vmem((ny, width, quarter), BF16),
         vmem((nx, width, quarter), BF16),
         vmem((2, slot, width), F32),

time: 57 us -> 55.9 us (0.981)
  Pallas kernels: 56.2 us -> 55.1 us
    pallas_call x1, Pallas kernels: 55.4 us -> 54.3 us  [local(): pl.pallas_call(functools.partial(layer_kernel, sizes), out_shape=(vmem((r...]
where the time goes in v5:
time: 55.9 us; the launch traced here: 55.8 us
  Pallas kernels  55.1 us (99%)
  between operations  0.64 us (1%)
    pallas_call x1, Pallas kernels, local(): pl.pallas_call(functools.partial(layer_kernel, sizes), out_shape=(vmem((r...  54.3 us

profile of v5, /device:TPU:1, one launch (start us, length us, event | category | flops | bytes accessed | tf_op | source)
XLA Modules:
  0.0 55.8 jit_solution(17354262194603999562)
XLA Ops:
  0.6 54.3 %prefill_layer.1 = (bf16[16,4096]{1,0:T(8,128)(2,1)S(1)}, f32[2,256,128]{2,1,0:T(8,128)S(1)}) custom-call(s32[64]{0:T(128)} %prefix_h.1, s32[2]{0:T(128)} %lengths_h.1, f32[8]{0:T(128)} %bias_h.1, f32[8]{0:T(128)} %rates_h.1, f32[8]{0:T(128)} %skip_h.1, bf16[256,256]{1,0:T(8,128)(2,1)} %x_h.1, bf16[256,256]{1,0:T(8,128)(2,1)} %z_h.1, ...), custom_call_target="tpu_custom_call" | custom-call | tf_op jit(solution)/shard_map/prefill_layer/pallas_call | solution.py:902
  55.0 0.8 %store_results.1 = (bf16[16,4096]{1,0:T(8,128)(2,1)}, f32[2,256,128]{2,1,0:T(8,128)}) custom-call(bf16[16,4096]{1,0:T(8,128)(2,1)S(1)} %get-tuple-element.6.mixed_v, f32[2,256,128]{2,1,0:T(8,128)S(1)} %get-tuple-element.7.final_v), custom_call_target="tpu_custom_call" | custom-call | tf_op jit(solution)/shard_map/store_results/pallas_call | solution.py:930

commit v6 on v5

--- a/solution.py
+++ b/solution.py
@@ -566,12 +566,13 @@
     ss_peers = grid_peers() + [(xi, yi, 1 - ci)]
     for xx, yy, cc in ss_peers:
         ss_copy(xx, yy, cc).start()
-    for d in (2, 1, 3, 0):
-        for dc in range(2):
-            if (d or dc) and d < ny:
-                va_copy((yi + d) % ny, (ci + dc) % 2).start()
-            if (d or dc) and d < nx:
-                vb_copy((xi + d) % nx, (ci + dc) % 2).start()
+    for d in (2, 1, 3):
+        if d < ny:
+            va_copy((yi + d) % ny, ci).start()
+        if d < nx:
+            vb_copy((xi + d) % nx, ci).start()
+    va_copy(yi, 1 - ci).start()
+    vb_copy(xi, 1 - ci).start()
     ss_recv[ci * nx + xi, yi] = ss_send[...]
     own_a = pltpu.make_async_copy(v_a.at[:, yi], r_a.at[ci, yi], own_sem.at[4])
     own_a.start()
@@ -582,6 +583,33 @@
         start_at, xc, b_low = saved[q]
         weighed = (xc * weighin[q]).astype(BF16)
         final_o[q] = ending[q] * start_at + dot_tn(weighed, b_low)
+
+    per_a = nx * rows_owner
+    per_b = ny * rows_owner
+
+    half = quarter // 2
+    x_order = x_peers()[::-1]
+    y_order = y_peers()[::-1]
+    if nx > 2:
+        x_order = [((xi + d) % nx, (ci + e) % 2) for d in (2, 1, 3) for e in range(2)]
+        x_order.append((xi, 1 - ci))
+    if ny > 2:
+        y_order = [((yi + d) % ny, (ci + e) % 2) for d in (2, 1, 3) for e in range(2)]
+        y_order.append((yi, 1 - ci))
+
+    def block_a(yy, cols):
+        lhs = jnp.concatenate(
+            [r_a[0, yy].reshape(per_a, width), r_a[1, yy].reshape(per_a, width)], axis=0
+        )
+        return jnp.dot(lhs, w_a[yy, :, cols], preferred_element_type=F32)
+
+    def block_b(at, cols):
+        xx = at
+        lhs = jnp.concatenate(
+            [r_b[0, xx].reshape(per_b, width), r_b[1, xx].reshape(per_b, width)], axis=0
+        )
+        col = jnp.concatenate([col_b[:, at : at + 1], col_b[:, nx + at : nx + at + 1]], axis=0)
+        return jnp.dot(lhs, w_b[xx, :, cols], preferred_element_type=F32) * col
 
     def wait_va(yy, cores):
         for cc in cores:
@@ -605,32 +633,23 @@
                 tensor_of(xx, yi),
             ).wait_recv()
 
-    per_a = nx * rows_owner
-    per_b = ny * rows_owner
-
-    half = quarter // 2
-    x_order = x_peers()[::-1]
-    y_order = y_peers()[::-1]
-    if nx > 2:
-        x_order = [((xi + d) % nx, (ci + e) % 2) for d in (2, 1, 3) for e in range(2)]
-        x_order.append((xi, 1 - ci))
-    if ny > 2:
-        y_order = [((yi + d) % ny, (ci + e) % 2) for d in (2, 1, 3) for e in range(2)]
-        y_order.append((yi, 1 - ci))
-
-    def block_a(yy, cols):
-        lhs = jnp.concatenate(
-            [r_a[0, yy].reshape(per_a, width), r_a[1, yy].reshape(per_a, width)], axis=0
-        )
-        return jnp.dot(lhs, w_a[yy, :, cols], preferred_element_type=F32)
-
-    def block_b(at, cols):
-        xx = at
-        lhs = jnp.concatenate(
-            [r_b[0, xx].reshape(per_b, width), r_b[1, xx].reshape(per_b, width)], axis=0
-        )
-        col = jnp.concatenate([col_b[:, at : at + 1], col_b[:, nx + at : nx + at + 1]], axis=0)
-        return jnp.dot(lhs, w_b[xx, :, cols], preferred_element_type=F32) * col
+    handed = []
+
+    def hand_on(buf, at, ssem, rsem):
+        ref = buf.at[ci, at]
+        copy = remote(ref, ref, ssem.at[1 - ci, at], rsem.at[ci, at], zi * 2 + 1 - ci, me_t)
+        copy.start()
+        handed.append(copy)
+
+    for d in (1, 3, 2):
+        if d < ny:
+            yy = (yi + d) % ny
+            wait_va(yy, (ci,))
+            hand_on(r_a, yy, va_send, va_recv)
+        if d < nx:
+            xx = (xi + d) % nx
+            wait_vb(xx, (ci,))
+            hand_on(r_b, xx, vb_send, vb_recv)
 
     for xx, yy, cc in ss_peers:
         remote(
@@ -667,8 +686,8 @@
         opp_y = (yi + 2) % ny
         weight_wait(w_a, opp_y, 0, fill, 8)
         weight_wait(w_a, opp_y, fill, fill, 9)
-    for yy, cc in y_peers():
-        wait_va(yy, (cc,))
+    for d in range(ny):
+        wait_va((yi + d) % ny, (1 - ci,))
     own_a.wait()
     own_b.wait()
     wait_vb(xi, (1 - ci,))
@@ -678,8 +697,8 @@
         opp_x = (xi + 2) % nx
         weight_wait(w_b, opp_x, 0, fill, 10)
         weight_wait(w_b, opp_x, fill, fill, 11)
-    for xx, cc in x_peers()[1:]:
-        wait_vb(xx, (cc,))
+    for d in range(1, nx):
+        wait_vb((xi + d) % nx, (1 - ci,))
 
     def oa_copy(h, xx, cc):
         return remote(
@@ -747,10 +766,14 @@
         copy.wait_send()
     for xx, yy, cc in ss_peers:
         ss_copy(xx, yy, cc).wait_send()
-    for yy, cc in y_peers():
-        va_copy(yy, cc).wait_send()
-    for xx, cc in x_peers():
-        vb_copy(xx, cc).wait_send()
+    for d in range(1, ny):
+        va_copy((yi + d) % ny, ci).wait_send()
+    for d in range(1, nx):
+        vb_copy((xi + d) % nx, ci).wait_send()
+    va_copy(yi, 1 - ci).wait_send()
+    vb_copy(xi, 1 - ci).wait_send()
+    for copy in handed:
+        copy.wait_send()
 
     for h in range(2):
         for xx, cc in x_peers():

time: 55.9 us -> 55.8 us (level)
  no operation moved by 1% of the time
where the time goes in v6:
time: 55.8 us; the launch traced here: 55.7 us
  Pallas kernels  55 us (99%)
  between operations  0.64 us (1%)
    pallas_call x1, Pallas kernels, local(): pl.pallas_call(functools.partial(layer_kernel, sizes), out_shape=(vmem((r...  54.2 us

profile of v6, /device:TPU:1, one launch (start us, length us, event | category | flops | bytes accessed | tf_op | source)
XLA Modules:
  0.0 55.7 jit_solution(2171940196282174563)
XLA Ops:
  0.6 54.2 %prefill_layer.1 = (bf16[16,4096]{1,0:T(8,128)(2,1)S(1)}, f32[2,256,128]{2,1,0:T(8,128)S(1)}) custom-call(s32[64]{0:T(128)} %prefix_h.1, s32[2]{0:T(128)} %lengths_h.1, f32[8]{0:T(128)} %bias_h.1, f32[8]{0:T(128)} %rates_h.1, f32[8]{0:T(128)} %skip_h.1, bf16[256,256]{1,0:T(8,128)(2,1)} %x_h.1, bf16[256,256]{1,0:T(8,128)(2,1)} %z_h.1, ...), custom_call_target="tpu_custom_call" | custom-call | tf_op jit(solution)/shard_map/prefill_layer/pallas_call | solution.py:925
  54.9 0.8 %store_results.1 = (bf16[16,4096]{1,0:T(8,128)(2,1)}, f32[2,256,128]{2,1,0:T(8,128)}) custom-call(bf16[16,4096]{1,0:T(8,128)(2,1)S(1)} %get-tuple-element.6.mixed_v, f32[2,256,128]{2,1,0:T(8,128)S(1)} %get-tuple-element.7.final_v), custom_call_target="tpu_custom_call" | custom-call | tf_op jit(solution)/shard_map/store_results/pallas_call | solution.py:953

commit v7 on v6

--- a/solution.py
+++ b/solution.py
@@ -564,8 +564,6 @@
         )
 
     ss_peers = grid_peers() + [(xi, yi, 1 - ci)]
-    for xx, yy, cc in ss_peers:
-        ss_copy(xx, yy, cc).start()
     for d in (2, 1, 3):
         if d < ny:
             va_copy((yi + d) % ny, ci).start()
@@ -573,6 +571,8 @@
             vb_copy((xi + d) % nx, ci).start()
     va_copy(yi, 1 - ci).start()
     vb_copy(xi, 1 - ci).start()
+    for xx, yy, cc in ss_peers:
+        ss_copy(xx, yy, cc).start()
     ss_recv[ci * nx + xi, yi] = ss_send[...]
     own_a = pltpu.make_async_copy(v_a.at[:, yi], r_a.at[ci, yi], own_sem.at[4])
     own_a.start()

time: 55.8 us -> 56.1 us (level)
  no operation moved by 1% of the time
where the time goes in v7:
time: 56.1 us; the launch traced here: 56 us
  Pallas kernels  55.3 us (99%)
  between operations  0.64 us (1%)
    pallas_call x1, Pallas kernels, local(): pl.pallas_call(functools.partial(layer_kernel, sizes), out_shape=(vmem((r...  54.6 us

profile of v7, /device:TPU:1, one launch (start us, length us, event | category | flops | bytes accessed | tf_op | source)
XLA Modules:
  0.0 56.0 jit_solution(10126932860687673748)
XLA Ops:
  0.6 54.6 %prefill_layer.1 = (bf16[16,4096]{1,0:T(8,128)(2,1)S(1)}, f32[2,256,128]{2,1,0:T(8,128)S(1)}) custom-call(s32[64]{0:T(128)} %prefix_h.1, s32[2]{0:T(128)} %lengths_h.1, f32[8]{0:T(128)} %bias_h.1, f32[8]{0:T(128)} %rates_h.1, f32[8]{0:T(128)} %skip_h.1, bf16[256,256]{1,0:T(8,128)(2,1)} %x_h.1, bf16[256,256]{1,0:T(8,128)(2,1)} %z_h.1, ...), custom_call_target="tpu_custom_call" | custom-call | tf_op jit(solution)/shard_map/prefill_layer/pallas_call | solution.py:925
  55.2 0.8 %store_results.1 = (bf16[16,4096]{1,0:T(8,128)(2,1)}, f32[2,256,128]{2,1,0:T(8,128)}) custom-call(bf16[16,4096]{1,0:T(8,128)(2,1)S(1)} %get-tuple-element.6.mixed_v, f32[2,256,128]{2,1,0:T(8,128)S(1)} %get-tuple-element.7.final_v), custom_call_target="tpu_custom_call" | custom-call | tf_op jit(solution)/shard_map/store_results/pallas_call | solution.py:953
